TPU v7x, 256 devices: a whole 4x4x8 slice. The times are simulated.
256 devices in a mesh: depth: 8 (over z_hi, core), seq: 32 (over x, y, z_lo).
Axes of the slice: x: 4, y: 4, z: 8 (z_hi: 4, z_lo: 2; z = z_hi * 2 + z_lo), core: 2. Of those that a mesh axis runs over, the one named last changes fastest.
Arguments:
- queries: bfloat16 [8, 4096, 4096], P('depth', 'seq'), may hold values from -27 to 27
- grad_out: bfloat16 [8, 4096, 4096], P('depth', 'seq'), may hold values from -48 to 48
- key_states: bfloat16 [4096, 4096], P('depth', 'seq'), may hold values from -3 to 3
- value_states: bfloat16 [4096, 4096], P('depth', 'seq'), may hold values from -6 to 6
- offsets: int32 [8], replicated, may hold values from 0 to 8, as said below
- windows: int32 [8], replicated, may hold values from 512 to 1024, as said below
Outputs:
- grad_queries: bfloat16 [8, 4096, 4096], P('depth', 'seq')
- grad_keys: bfloat16 [4096, 4096], P('depth', 'seq')
- grad_values: bfloat16 [4096, 4096], P('depth', 'seq')
Inputs may be any that keep to these rules, and one draw needn't show every extreme that they name: `windows`: one depth's window is exactly 1024. `offsets`: one depth's offset is exactly 8.
All inputs are finite; a program needn't handle non-finite values.
Results may differ from a plain program's by a relative error of at most 0.033.
Values may be sent and summed in bfloat16 or wider, within the bound.
A program may use at most 64 MiB of HBM per device.

v0:
```python
import math

import jax
import jax.numpy as jnp
from jax import lax
from jax.sharding import PartitionSpec as P

HEAD_DIM = 128
WIN = 1024
OFF_MAX = 8


def allowed_mask(query_pos, key_pos, shift_now, span_now, seq_total):
    query_col = query_pos[:, None]
    key_row = key_pos[None, :]
    inside = (key_row >= 0) & (key_row < seq_total) & (query_col >= 0) & (query_col < seq_total)
    return (
        inside & (key_row <= query_col + shift_now) & (key_row > query_col + shift_now - span_now)
    )


def head_scores(query_blk, key_blk):
    scaling = 1.0 / math.sqrt(HEAD_DIM)
    return (
        jnp.einsum("qhd,khd->hqk", query_blk, key_blk, preferred_element_type=jnp.float32) * scaling
    )


def on_device(queries, grad_out, key_states, value_states, offsets, windows):
    scaling = 1.0 / math.sqrt(HEAD_DIM)
    depth_id = lax.axis_index("depth")
    picked = jnp.arange(offsets.shape[0], dtype=jnp.int32) == depth_id
    shift_now = jnp.sum(jnp.where(picked, offsets, 0))
    span_now = jnp.sum(jnp.where(picked, windows, 0))
    tok_rows = queries.shape[1]
    model_width = queries.shape[2]
    query_heads, grad_heads = (
        lax.all_to_all(
            queries.reshape(tok_rows, model_width), "seq", split_axis=1, concat_axis=0, tiled=True
        ),
        lax.all_to_all(
            grad_out.reshape(tok_rows, model_width), "seq", split_axis=1, concat_axis=0, tiled=True
        ),
    )
    key_all, value_all = (
        lax.all_gather(key_states, "depth", axis=0, tiled=True),
        lax.all_gather(value_states, "depth", axis=0, tiled=True),
    )
    seq_total = query_heads.shape[0]
    width = query_heads.shape[1]
    head_count = width // HEAD_DIM
    depth_rows = seq_total // lax.axis_size("depth")
    block_len = min(512, depth_rows)
    blocks = seq_total // block_len
    span_keys = block_len + WIN
    query3 = query_heads.reshape(seq_total, head_count, HEAD_DIM)
    grad3 = grad_heads.reshape(seq_total, head_count, HEAD_DIM)
    key3 = key_all.reshape(seq_total, head_count, HEAD_DIM)
    value3 = value_all.reshape(seq_total, head_count, HEAD_DIM)
    widths = ((WIN, OFF_MAX + 1), (0, 0), (0, 0))
    key_pad = jnp.pad(key3, widths)
    value_pad = jnp.pad(value3, widths)

    def block_grads(number):
        first_row = number * block_len
        key_first = first_row + shift_now + 1
        query_blk = lax.dynamic_slice_in_dim(query3, first_row, block_len, 0)
        grad_blk = lax.dynamic_slice_in_dim(grad3, first_row, block_len, 0)
        key_blk = lax.dynamic_slice_in_dim(key_pad, key_first, span_keys, 0)
        value_blk = lax.dynamic_slice_in_dim(value_pad, key_first, span_keys, 0)
        scores = head_scores(query_blk, key_blk)
        query_pos = first_row + jnp.arange(block_len, dtype=jnp.int32)
        key_pos = key_first - WIN + jnp.arange(span_keys, dtype=jnp.int32)
        allowed = allowed_mask(query_pos, key_pos, shift_now, span_now, seq_total)
        masked = jnp.where(allowed[None], scores, -jnp.inf)
        highest = jnp.max(masked, axis=2, keepdims=True)
        log_total = highest + jnp.log(jnp.sum(jnp.exp(masked - highest), axis=2, keepdims=True))
        probs = jnp.exp(masked - log_total)
        weights = probs.astype(jnp.bfloat16)
        grad_probs = jnp.einsum(
            "qhd,khd->hqk", grad_blk, value_blk, preferred_element_type=jnp.float32
        )
        row_dot = jnp.sum(weights.astype(jnp.float32) * grad_probs, axis=2, keepdims=True)
        grad_scores = (probs * (grad_probs - row_dot)).astype(jnp.bfloat16)
        grad_query = (
            jnp.einsum("hqk,khd->qhd", grad_scores, key_blk, preferred_element_type=jnp.float32)
            * scaling
        )
        return (
            grad_query,
            grad_scores,
            weights,
            query_blk,
            grad_blk,
            key_first,
            log_total[:, :, 0],
            row_dot[:, :, 0],
        )

    def accumulate(carry, number):
        key_acc, value_acc = carry
        grad_query, grad_scores, weights, query_blk, grad_blk, key_first, log_total, row_dot = (
            block_grads(number)
        )
        key_term = (
            jnp.einsum("hqk,qhd->khd", grad_scores, query_blk, preferred_element_type=jnp.float32)
            * scaling
        )
        value_term = jnp.einsum(
            "hqk,qhd->khd", weights, grad_blk, preferred_element_type=jnp.float32
        )
        root = jnp.zeros((), jnp.int32)
        place = (key_first, root, root)
        key_acc = lax.dynamic_update_slice(
            key_acc, lax.dynamic_slice(key_acc, place, key_term.shape) + key_term, place
        )
        value_acc = lax.dynamic_update_slice(
            value_acc, lax.dynamic_slice(value_acc, place, value_term.shape) + value_term, place
        )
        return ((key_acc, value_acc), grad_query)

    start_acc = jnp.zeros((seq_total + WIN + OFF_MAX + 1, head_count, HEAD_DIM), jnp.float32)
    (key_acc, value_acc), grad_rows = lax.scan(
        accumulate, (start_acc, start_acc), jnp.arange(blocks, dtype=jnp.int32)
    )
    stacked = jnp.concatenate(
        [
            key_acc[WIN : WIN + seq_total].reshape(seq_total, width),
            value_acc[WIN : WIN + seq_total].reshape(seq_total, width),
        ],
        axis=1,
    )
    summed = lax.psum_scatter(
        stacked.astype(jnp.bfloat16), "depth", scatter_dimension=0, tiled=True
    ).astype(jnp.float32)
    grad_query = grad_rows.reshape(seq_total, width).astype(jnp.bfloat16)
    grad_back = lax.all_to_all(grad_query, "seq", split_axis=0, concat_axis=1, tiled=True)
    grad_keys = summed[:, :width].astype(jnp.bfloat16)
    grad_values = summed[:, width:].astype(jnp.bfloat16)
    return (grad_back.reshape(1, tok_rows, model_width), grad_keys, grad_values)


def solution(mesh):
    in_specs = (
        P("depth", "seq", None),
        P("depth", "seq", None),
        P("depth", "seq"),
        P("depth", "seq"),
        P(),
        P(),
    )
    out_specs = (P("depth", "seq", None), P("depth", "seq"), P("depth", "seq"))
    return jax.shard_map(
        on_device, mesh=mesh, in_specs=in_specs, out_specs=out_specs, check_vma=False
    )
```

profile of v0, /device:TPU:1, one launch (start us, length us, event | category | flops | bytes accessed | tf_op | source)
XLA Modules:
  0.0 419.3 jit_solution(9278927847605782534)
XLA Ops:
  9.5 9.4 %all-to-all-start = ((bf16[128,32,128]{0,2,1:T(8,128)(2,1)}), bf16[128,32,128]{0,2,1:T(8,128)(2,1)S(1)}, u32[]{:S(2)}, u32[]{:S(2)}) async-start(bf16[128,32,128]{0,2,1:T(8,128)(2,1)} %bitcast.12), calls=%async_computation | async-start | bytes 2097152 | tf_op jit(solution)/shard_map/all_to_all | solution.py:38
  21.0 14.6 %all-to-all-done = bf16[128,32,128]{0,2,1:T(8,128)(2,1)S(1)} async-done(((bf16[128,32,128]{0,2,1:T(8,128)(2,1)}), bf16[128,32,128]{0,2,1:T(8,128)(2,1)S(1)}, u32[]{:S(2)}, u32[]{:S(2)}) %all-to-all-start) | async-done | bytes 1048608 | tf_op jit(solution)/shard_map/all_to_all | solution.py:38
  35.6 3.9 all-to-all-start.1
  41.0 14.6 %all-gather.3.cloned.1.call-done = bf16[4096,128]{1,0:T(8,128)(2,1)} async-done(((bf16[512,128]{1,0:T(8,128)(2,1)}), bf16[4096,128]{1,0:T(8,128)(2,1)}) %all-gather.3.cloned.1.call-update) | async-done | bytes 1048592 | tf_op jit(solution)/shard_map/all_gather | solution.py:46
  57.9 28.6 %all-gather.5.cloned.1.call-done = bf16[4096,128]{1,0:T(8,128)(2,1)} async-done(((bf16[512,128]{1,0:T(8,128)(2,1)}), bf16[4096,128]{1,0:T(8,128)(2,1)}) %all-gather.5.cloned.1.call-update) | async-done | bytes 1048592 | tf_op jit(solution)/shard_map/all_gather | solution.py:47
  95.0 267.0 %while.18 = (s32[]{:T(128)}, f32[5129,1,128]{2,0,1:T(8,128)}, f32[5129,1,128]{2,0,1:T(8,128)}, bf16[8,512,1,128]{3,1,0,2:T(8,128)(2,1)}, s32[8]{0:T(128)S(1)}, /...) while((s32[]{:T(128)}, f32[5129,1,128]{2,0,1:T(8,128)}, ...), condition=%wide.region_6.7_spmd, body=%wide.region_2.6_spmd.sunk | while | flops 1024665088 | bytes 51167096 | solution.py:123
  98.2 2.6 fusion.58
  101.3 2.6 constant_dynamic-slice_fusion.3
  106.3 2.8 fusion.60
  111.4 3.6 dynamic_update_slice.34
  122.5 3.5 dynamic_update_slice.33
  131.6 2.6 fusion.58
  134.8 2.6 constant_dynamic-slice_fusion.3
  139.7 2.8 fusion.60
  144.9 3.6 dynamic_update_slice.34
  155.9 3.5 dynamic_update_slice.33
  165.1 2.6 fusion.58
  168.3 2.6 constant_dynamic-slice_fusion.3
  173.2 2.8 fusion.60
  178.4 3.6 dynamic_update_slice.34
  189.4 3.5 dynamic_update_slice.33
  198.6 2.6 fusion.58
  201.7 2.6 constant_dynamic-slice_fusion.3
  206.7 2.8 fusion.60
  211.8 3.6 dynamic_update_slice.34
  222.9 3.5 dynamic_update_slice.33
  232.0 2.6 fusion.58
  235.2 2.6 constant_dynamic-slice_fusion.3
  240.1 2.8 fusion.60
  245.3 3.6 dynamic_update_slice.34
  256.3 3.5 dynamic_update_slice.33
  265.5 2.6 fusion.58
  268.7 2.6 constant_dynamic-slice_fusion.3
  273.6 2.8 fusion.60
  278.8 3.6 dynamic_update_slice.34
  289.8 3.5 dynamic_update_slice.33
  299.0 2.6 fusion.58
  302.1 2.6 constant_dynamic-slice_fusion.3
  307.1 2.8 fusion.60
  312.2 3.6 dynamic_update_slice.34
  323.3 3.5 dynamic_update_slice.33
  332.4 2.6 fusion.58
  335.6 2.6 constant_dynamic-slice_fusion.3
  340.5 2.8 fusion.60
  345.7 3.3 dynamic_update_slice.34
  356.4 3.1 dynamic_update_slice.33
  367.0 32.1 %all_to_all.45 = bf16[32,128,128]{2,1,0:T(8,128)(2,1)S(1)} all-to-all(bf16[32,128,128]{2,1,0:T(8,128)(2,1)S(1)} %bitcast.94), channel_id=1, replica_groups=mesh['depth'=8,'seq'=32] {'seq'}, dimensions={0} | all-to-all | bytes 2097152 | tf_op jit(solution)/shard_map/all_to_all | solution.py:137
  401.1 10.0 %reduce-scatter.2.cloned.1.call-done = bf16[512,256]{1,0:T(8,128)(2,1)} async-done(((bf16[4096,256]{1,0:T(8,128)(2,1)}), bf16[512,256]{1,0:T(8,128)(2,1)}) %reduce-scatter.2.cloned.1.call-update) | async-done | bytes 262160 | tf_op jit(solution)/shard_map/reduce_scatter | solution.py:133
  (184 shorter events, 160.9 us)
Async XLA Ops:
  7.2 12.5 %copy-start.1 = (bf16[1,128,4096]{2,1,0:T(8,128)(2,1)S(1)}, bf16[1,128,4096]{2,1,0:T(8,128)(2,1)}, u32[]{:S(2)}) copy-start(bf16[1,128,4096]{2,1,0:T(8,128)(2,1)} %param.9) | copy-start | bytes 3145732
  9.5 30.8 %copy-start.3 = (s32[8]{0:T(128)S(1)}, s32[8]{0:T(128)}, u32[]{:S(2)}) copy-start(s32[8]{0:T(128)} %param.12) | copy-start | bytes 100
  9.5 30.8 %copy-start.4 = (s32[8]{0:T(128)S(1)}, s32[8]{0:T(128)}, u32[]{:S(2)}) copy-start(s32[8]{0:T(128)} %param.13) | copy-start | bytes 100
  9.5 26.0 %all-to-all-start = ((bf16[128,32,128]{0,2,1:T(8,128)(2,1)}), bf16[128,32,128]{0,2,1:T(8,128)(2,1)S(1)}, u32[]{:S(2)}, u32[]{:S(2)}) async-start(bf16[128,32,128]{0,2,1:T(8,128)(2,1)} %bitcast.12), calls=%async_computation | async-start | bytes 2097152 | tf_op jit(solution)/shard_map/all_to_all | solution.py:38
  18.9 36.6 %all-gather.3.cloned.1.call-start = ((), (), s32[]{:S(2)}) async-start(), calls=%async_computation.4 | async-start | bytes 1179648 | tf_op jit(solution)/shard_map/all_gather | solution.py:46
  35.6 54.7 %all-to-all-start.1 = ((bf16[128,32,128]{0,2,1:T(8,128)(2,1)}), bf16[128,32,128]{0,2,1:T(8,128)(2,1)S(1)}, u32[]{:S(2)}, u32[]{:S(2)}) async-start(bf16[128,32,128]{0,2,1:T(8,128)(2,1)} %bitcast.16), calls=%async_computation.1 | async-start | bytes 2097152 | tf_op jit(solution)/shard_map/all_to_all | solution.py:41
  39.5 47.0 %all-gather.5.cloned.1.call-start = ((), (), s32[]{:S(2)}) async-start(), calls=%async_computation.5 | async-start | bytes 1179648 | tf_op jit(solution)/shard_map/all_gather | solution.py:47
  40.3 370.8 %reduce-scatter.2.cloned.1.call-start = ((), (), s32[]{:S(2)}) async-start(), calls=%async_computation.6 | async-start | bytes 2359296 | tf_op jit(solution)/shard_map/reduce_scatter | solution.py:133
  120.2 5.8 %copy-start = (bf16[512,1536]{1,0:T(8,128)(2,1)S(1)}, bf16[512,1536]{1,0:T(8,128)(2,1)}, u32[]{:S(2)}) copy-start(bf16[512,1536]{1,0:T(8,128)(2,1)} %multiply_convert_fusion.2) | copy-start | bytes 4718596 | tf_op jit(solution)/shard_map/while
  153.7 5.8 %copy-start = (bf16[512,1536]{1,0:T(8,128)(2,1)S(1)}, bf16[512,1536]{1,0:T(8,128)(2,1)}, u32[]{:S(2)}) copy-start(bf16[512,1536]{1,0:T(8,128)(2,1)} %multiply_convert_fusion.2) | copy-start | bytes 4718596 | tf_op jit(solution)/shard_map/while
  187.1 5.8 %copy-start = (bf16[512,1536]{1,0:T(8,128)(2,1)S(1)}, bf16[512,1536]{1,0:T(8,128)(2,1)}, u32[]{:S(2)}) copy-start(bf16[512,1536]{1,0:T(8,128)(2,1)} %multiply_convert_fusion.2) | copy-start | bytes 4718596 | tf_op jit(solution)/shard_map/while
  220.6 5.8 %copy-start = (bf16[512,1536]{1,0:T(8,128)(2,1)S(1)}, bf16[512,1536]{1,0:T(8,128)(2,1)}, u32[]{:S(2)}) copy-start(bf16[512,1536]{1,0:T(8,128)(2,1)} %multiply_convert_fusion.2) | copy-start | bytes 4718596 | tf_op jit(solution)/shard_map/while
  254.1 5.8 %copy-start = (bf16[512,1536]{1,0:T(8,128)(2,1)S(1)}, bf16[512,1536]{1,0:T(8,128)(2,1)}, u32[]{:S(2)}) copy-start(bf16[512,1536]{1,0:T(8,128)(2,1)} %multiply_convert_fusion.2) | copy-start | bytes 4718596 | tf_op jit(solution)/shard_map/while
  287.6 5.8 %copy-start = (bf16[512,1536]{1,0:T(8,128)(2,1)S(1)}, bf16[512,1536]{1,0:T(8,128)(2,1)}, u32[]{:S(2)}) copy-start(bf16[512,1536]{1,0:T(8,128)(2,1)} %multiply_convert_fusion.2) | copy-start | bytes 4718596 | tf_op jit(solution)/shard_map/while
  321.0 5.8 %copy-start = (bf16[512,1536]{1,0:T(8,128)(2,1)S(1)}, bf16[512,1536]{1,0:T(8,128)(2,1)}, u32[]{:S(2)}) copy-start(bf16[512,1536]{1,0:T(8,128)(2,1)} %multiply_convert_fusion.2) | copy-start | bytes 4718596 | tf_op jit(solution)/shard_map/while
  354.1 5.4 %copy-start = (bf16[512,1536]{1,0:T(8,128)(2,1)S(1)}, bf16[512,1536]{1,0:T(8,128)(2,1)}, u32[]{:S(2)}) copy-start(bf16[512,1536]{1,0:T(8,128)(2,1)} %multiply_convert_fusion.2) | copy-start | bytes 4718596 | tf_op jit(solution)/shard_map/while
  365.4 1.6 copy-start.2
Sparse Core Ops, SparseCore 0:
  21.6 33.8 all-gather.2
  57.4 29.0 all-gather.4
  367.1 43.9 reduce-scatter.1
where the time goes:
time: 425 us; the launch traced here: 419 us
  local copies, waits for them, and re-layouts  160 us (38%)
  matrix products  87.5 us (21%)
  waiting for transfers between devices  69.1 us (16%)
  blocking collectives  32.1 us (8%)
  other arithmetic  32 us (8%)
  between operations  13.8 us (3%)
  starting transfers between devices  13.4 us (3%)
  loops' own time  10.9 us (3%)
    dynamic_update_slice x16, local copies, waits for them, and re-layouts, accumulate(): lax.dynamic_update_slice(value_acc, lax.dynamic_slice(value_acc, place, v...  46.9 us
    dynamic_slice x16, local copies, waits for them, and re-layouts, accumulate(): lax.dynamic_slice(value_acc, place, value_term.shape) + value_term  39.6 us
    all_to_all x1, blocking collectives, on_device(): lax.all_to_all(grad_query, 'seq', split_axis=0, concat_axis=1, tiled=True)  32.1 us
    dynamic_update_slice x16, local copies, waits for them, and re-layouts, accumulate(): lax.dynamic_update_slice(key_acc, lax.dynamic_slice(key_acc, place, key_t...  29.7 us
    all_gather x1, waiting for transfers between devices, on_device(): lax.all_gather(value_states, 'depth', axis=0, tiled=True)  28.6 us
    dot_general x8, matrix products, accumulate(): jnp.einsum('hqk,qhd->khd', weights, grad_blk, preferred_element_type=jnp....  22.7 us
    dot_general x8, matrix products, head_scores(): jnp.einsum('qhd,khd->hqk', query_blk, key_blk, preferred_element_type=jnp...  20.5 us
    dot_general x8, matrix products, accumulate(): jnp.einsum('hqk,qhd->khd', grad_scores, query_blk, preferred_element_type...  15.9 us
  transfers between devices with their start and end apart: 5, of which 4 were waited for; matrix products, arithmetic and copies ran while one was open for 2% of the time, Pallas kernels for 0%

commit v1 on v0

v1 whole, which is shorter than its diff:
```python
import functools
import math

import jax
import jax.numpy as jnp
from jax import lax
from jax.experimental import pallas as pl
from jax.experimental.pallas import tpu as pltpu
from jax.sharding import PartitionSpec as P

HEAD_DIM = 128
WIN = 1024
TILE = 256
SPAN = WIN + TILE
NEG = -1e30
SCALE = 1.0 / math.sqrt(HEAD_DIM)
SCALE2 = SCALE * math.log2(math.e)


def dot_t(a, b):
    return lax.dot_general(a, b, (((1,), (1,)), ((), ())), preferred_element_type=jnp.float32)


def attention_kernel(
    scal_ref, q_ref, g_ref, k_ref, v_ref, dq_ref, dkv_ref, stage, ks, vs, kt, dks, dvs, s_scr, dp_scr
):
    shift = scal_ref[0]
    span = scal_ref[1]
    rows = q_ref.shape[0]
    total = rows + WIN

    stage[pl.ds(rows, 16), :] = jnp.zeros((16, HEAD_DIM), jnp.float32)
    for src, dst in ((k_ref, ks), (v_ref, vs)):
        dst[pl.ds(0, WIN - 16), :] = jnp.zeros((WIN - 16, HEAD_DIM), jnp.bfloat16)
        stage[pl.ds(0, rows), :] = src[...].astype(jnp.float32)
        dst[pl.ds(WIN, rows), :] = stage[pl.ds(shift, rows), :].astype(jnp.bfloat16)
        head = stage[pl.ds(0, 16), :]
        wide = jnp.concatenate([jnp.zeros((16, HEAD_DIM), jnp.float32), head], axis=0)
        stage[pl.ds(0, 32), :] = wide
        dst[pl.ds(WIN - 16, 16), :] = stage[pl.ds(shift, 16), :].astype(jnp.bfloat16)
    for c in range(total // TILE):
        kt[:, pl.ds(c * TILE, TILE)] = ks[pl.ds(c * TILE, TILE), :].T
    dks[...] = jnp.zeros_like(dks)
    dvs[...] = jnp.zeros_like(dvs)

    blocks = SPAN // TILE
    gap = lax.broadcasted_iota(jnp.int32, (TILE, TILE), 0) - lax.broadcasted_iota(
        jnp.int32, (TILE, TILE), 1
    )
    row = lax.broadcasted_iota(jnp.int32, (TILE, TILE), 0)

    def tile(t, carry):
        first = pl.multiple_of(t * TILE, TILE)
        q = q_ref[pl.ds(first, TILE), :]
        g = g_ref[pl.ds(first, TILE), :]
        high = jnp.full((1, TILE), NEG, jnp.float32)
        for b in range(blocks):
            at = pl.multiple_of(first + b * TILE, TILE)
            s = dot_t(ks[pl.ds(at, TILE), :], q)
            keep = gap > (WIN - b * TILE) - span
            if b == blocks - 1:
                keep = keep & (gap <= 0)
            pos = row + (at + shift - WIN)
            keep = keep & (pos >= 0) & (pos < rows)
            s = jnp.where(keep, s, NEG)
            s_scr[pl.ds(b * TILE, TILE), :] = s
            high = jnp.maximum(high, jnp.max(s, axis=0, keepdims=True))
        total_e = jnp.zeros((1, TILE), jnp.float32)
        total_d = jnp.zeros((1, TILE), jnp.float32)
        for b in range(blocks):
            at = pl.multiple_of(first + b * TILE, TILE)
            dp = dot_t(vs[pl.ds(at, TILE), :], g)
            e = jnp.exp2((s_scr[pl.ds(b * TILE, TILE), :] - high) * SCALE2)
            total_e += jnp.sum(e, axis=0, keepdims=True)
            total_d += jnp.sum(e * dp, axis=0, keepdims=True)
            s_scr[pl.ds(b * TILE, TILE), :] = e
            dp_scr[pl.ds(b * TILE, TILE), :] = dp
        inv = 1.0 / total_e
        rowdot = total_d * inv
        dqt = jnp.zeros((HEAD_DIM, TILE), jnp.float32)
        for b in range(blocks):
            at = pl.multiple_of(first + b * TILE, TILE)
            p = s_scr[pl.ds(b * TILE, TILE), :] * inv
            ds = (p * (dp_scr[pl.ds(b * TILE, TILE), :] - rowdot)).astype(jnp.bfloat16)
            pb = p.astype(jnp.bfloat16)
            dvs[pl.ds(at, TILE), :] += jnp.dot(pb, g, preferred_element_type=jnp.float32)
            dks[pl.ds(at, TILE), :] += jnp.dot(ds, q, preferred_element_type=jnp.float32)
            dqt += jnp.dot(kt[:, pl.ds(at, TILE)], ds, preferred_element_type=jnp.float32)
        dq_ref[pl.ds(first, TILE), :] = (dqt.T * SCALE).astype(jnp.bfloat16)
        return carry

    lax.fori_loop(0, rows // TILE, tile, 0)

    dkv_ref[:, :HEAD_DIM] = (dks[pl.ds(WIN - shift, rows), :] * SCALE).astype(jnp.bfloat16)
    dkv_ref[:, HEAD_DIM:] = dvs[pl.ds(WIN - shift, rows), :].astype(jnp.bfloat16)


def attention_backward(scalars, q, g, k, v):
    rows = q.shape[0]
    vmem = pl.BlockSpec(memory_space=pltpu.VMEM)
    return pl.pallas_call(
        attention_kernel,
        out_shape=(
            jax.ShapeDtypeStruct((rows, HEAD_DIM), jnp.bfloat16),
            jax.ShapeDtypeStruct((rows, 2 * HEAD_DIM), jnp.bfloat16),
        ),
        in_specs=[pl.BlockSpec(memory_space=pltpu.SMEM)] + [vmem] * 4,
        out_specs=(vmem, vmem),
        scratch_shapes=[
            pltpu.VMEM((rows + 16, HEAD_DIM), jnp.float32),
            pltpu.VMEM((rows + WIN, HEAD_DIM), jnp.bfloat16),
            pltpu.VMEM((rows + WIN, HEAD_DIM), jnp.bfloat16),
            pltpu.VMEM((HEAD_DIM, rows + WIN), jnp.bfloat16),
            pltpu.VMEM((rows + WIN, HEAD_DIM), jnp.float32),
            pltpu.VMEM((rows + WIN, HEAD_DIM), jnp.float32),
            pltpu.VMEM((SPAN, TILE), jnp.float32),
            pltpu.VMEM((SPAN, TILE), jnp.float32),
        ],
        compiler_params=pltpu.CompilerParams(vmem_limit_bytes=48 << 20),
    )(scalars, q, g, k, v)


def on_device(queries, grad_out, key_states, value_states, offsets, windows):
    depth_id = lax.axis_index("depth")
    picked = jnp.arange(offsets.shape[0], dtype=jnp.int32) == depth_id
    shift_now = jnp.sum(jnp.where(picked, offsets, 0))
    span_now = jnp.sum(jnp.where(picked, windows, 0))
    scalars = jnp.stack([shift_now, span_now])
    tok_rows = queries.shape[1]
    model_width = queries.shape[2]
    q, g = (
        lax.all_to_all(a.reshape(tok_rows, model_width), "seq", split_axis=1, concat_axis=0, tiled=True)
        for a in (queries, grad_out)
    )
    k, v = (lax.all_gather(a, "depth", axis=0, tiled=True) for a in (key_states, value_states))
    dq, dkv = attention_backward(scalars, q, g, k, v)
    summed = lax.psum_scatter(dkv, "depth", scatter_dimension=0, tiled=True)
    back = lax.all_to_all(dq, "seq", split_axis=0, concat_axis=1, tiled=True)
    return (
        back.reshape(1, tok_rows, model_width),
        summed[:, :HEAD_DIM],
        summed[:, HEAD_DIM:],
    )


def solution(mesh):
    in_specs = (
        P("depth", "seq", None),
        P("depth", "seq", None),
        P("depth", "seq"),
        P("depth", "seq"),
        P(),
        P(),
    )
    out_specs = (P("depth", "seq", None), P("depth", "seq"), P("depth", "seq"))
    return jax.shard_map(
        on_device, mesh=mesh, in_specs=in_specs, out_specs=out_specs, check_vma=False
    )
```

time: 425 us -> 174 us (0.41)
  local copies, waits for them, and re-layouts: 160 us -> 10.6 us
  matrix products: 87.5 us -> 0 us
  other arithmetic: 32 us -> 2 us
  Pallas kernels: 0 us -> 29.8 us
  loops' own time: 10.9 us -> 0 us
    dot_general x40 -> x0, matrix products: 87.5 us -> none  [the longest x8 22.7 us: accumulate(): jnp.einsum('hqk,qhd->khd', weights, grad_blk, preferred_element_type=jnp....]
    dynamic_update_slice x48 -> x0, local copies, waits for them, and re-layouts: 82.9 us -> none  [the longest x16 46.9 us: accumulate(): lax.dynamic_update_slice(value_acc, lax.dynamic_slice(value_acc, place, v...]
    dynamic_slice x32 -> x0, local copies, waits for them, and re-layouts: 55.9 us -> none  [the longest x16 39.6 us: accumulate(): lax.dynamic_slice(value_acc, place, value_term.shape) + value_term]
    pallas_call x0 -> x1, Pallas kernels: none -> 29.8 us  [attention_backward(): pl.pallas_call(attention_kernel, out_shape=(jax.ShapeDtypeStruct((rows, H...]
    convert_element_type x8 -> x0, other arithmetic: 15.3 us -> none  [block_grads(): grad_scores = (probs * (grad_probs - row_dot)).astype(jnp.bfloat16)]
    another operation x1 -> x0, loops' own time: 10.9 us -> none  [on_device(): lax.scan(accumulate, (start_acc, start_acc), jnp.arange(blocks, dtype=jnp...]
    add x24 -> x0, other arithmetic: 9.78 us -> none  [the longest x8 9.67 us: allowed_mask(): query_col + shift_now]
    pad x2 -> x0, local copies, waits for them, and re-layouts: 4.89 us -> none  [the longest x1 2.49 us: on_device(): value_pad = jnp.pad(value3, widths)]
  transfers between devices with their start and end apart: 5 -> 5, of which waited for: 4 -> 4; matrix products, arithmetic and copies ran while one was open for 2% -> 3% of each run, Pallas kernels for 0% -> 0%
where the time goes in v1:
time: 174 us; the launch traced here: 171 us
  waiting for transfers between devices  69.7 us (40%)
  blocking collectives  32.2 us (19%)
  Pallas kernels  29.8 us (17%)
  between operations  13.8 us (8%)
  starting transfers between devices  13.3 us (8%)
  local copies, waits for them, and re-layouts  10.6 us (6%)
  other arithmetic  2 us (1%)
    all_gather x2, waiting for transfers between devices, on_device(): lax.all_gather(a, 'depth', axis=0, tiled=True)  44.2 us
    all_to_all x1, blocking collectives, on_device(): back = lax.all_to_all(dq, 'seq', split_axis=0, concat_axis=1, tiled=True)  32.2 us
    pallas_call x1, Pallas kernels, attention_backward(): pl.pallas_call(attention_kernel, out_shape=(jax.ShapeDtypeStruct((rows, H...  29.8 us
    all_to_all x2, waiting for transfers between devices, on_device(): lax.all_to_all(a.reshape(tok_rows, model_width), 'seq', split_axis=1, con...  14.3 us
    all_to_all x2, starting transfers between devices, on_device(): lax.all_to_all(a.reshape(tok_rows, model_width), 'seq', split_axis=1, con...  13.2 us
    reduce_scatter x1, waiting for transfers between devices, on_device(): summed = lax.psum_scatter(dkv, 'depth', scatter_dimension=0, tiled=True)  9.9 us
    unnamed x12, local copies, waits for them, and re-layouts  4.16 us
  transfers between devices with their start and end apart: 5, of which 4 were waited for; matrix products, arithmetic and copies ran while one was open for 3% of the time, Pallas kernels for 0%

profile of v1, /device:TPU:1, one launch (start us, length us, event | category | flops | bytes accessed | tf_op | source)
XLA Modules:
  0.0 171.3 jit_solution(16821017590259911606)
XLA Ops:
  7.2 1.4 copy.12
  8.6 0.0 copy-start.2
  8.6 1.4 copy.9
  10.0 9.2 %all-to-all-start = ((bf16[128,32,128]{2,0,1:T(8,128)(2,1)}), bf16[128,32,128]{2,0,1:T(8,128)(2,1)S(1)}, u32[]{:S(2)}, u32[]{:S(2)}) async-start(bf16[128,32,128]{2,0,1:T(8,128)(2,1)} %copy.9), calls=%async_computation | async-start | bytes 2097152 | tf_op jit(solution)/shard_map/all_to_all | solution.py:132
  19.2 0.0 all-gather.3.cloned.1.call-start
  19.3 0.7 all-gather.3.cloned.1.call-update
  20.0 0.0 copy-done.2
  20.0 0.2 copy.13
  20.2 0.0 copy-start.3
  20.3 0.0 copy-start.4
  20.3 1.4 copy.10
  21.6 14.3 %all-to-all-done = bf16[128,32,128]{2,0,1:T(8,128)(2,1)S(1)} async-done(((bf16[128,32,128]{2,0,1:T(8,128)(2,1)}), bf16[128,32,128]{2,0,1:T(8,128)(2,1)S(1)}, u32[]{:S(2)}, u32[]{:S(2)}) %all-to-all-start) | async-done | bytes 1048608 | tf_op jit(solution)/shard_map/all_to_all | solution.py:132
  35.9 3.9 %all-to-all-start.1 = ((bf16[128,32,128]{2,0,1:T(8,128)(2,1)}), bf16[128,32,128]{2,0,1:T(8,128)(2,1)S(1)}, u32[]{:S(2)}, u32[]{:S(2)}) async-start(bf16[128,32,128]{2,0,1:T(8,128)(2,1)} %copy.10), calls=%async_computation.1 | async-start | bytes 2097152 | tf_op jit(solution)/shard_map/all_to_all | solution.py:132
  39.9 0.0 all-gather.5.cloned.1.call-start
  39.9 0.7 all-gather.5.cloned.1.call-update
  40.6 0.0 reduce-scatter.2.cloned.1.call-start
  40.7 0.0 copy-done.3
  40.7 0.0 copy-done.4
  40.7 0.6 fusion
  41.3 1.4 pad_add_fusion.scal_ref
  42.7 13.1 %all-gather.3.cloned.1.call-done.k_ref = bf16[4096,128]{1,0:T(8,128)(2,1)} async-done(((bf16[512,128]{1,0:T(8,128)(2,1)}), bf16[4096,128]{1,0:T(8,128)(2,1)}) %all-gather.3.cloned.1.call-update) | async-done | bytes 1048592 | tf_op jit(solution)/shard_map/all_gather | solution.py:135
  55.8 31.1 %all-gather.5.cloned.1.call-done.v_ref = bf16[4096,128]{1,0:T(8,128)(2,1)} async-done(((bf16[512,128]{1,0:T(8,128)(2,1)}), bf16[4096,128]{1,0:T(8,128)(2,1)}) %all-gather.5.cloned.1.call-update) | async-done | bytes 1048592 | tf_op jit(solution)/shard_map/all_gather | solution.py:135
  86.9 0.0 all-to-all-done.1
  86.9 0.0 copy-start
  86.9 1.2 copy-done
  88.1 0.0 copy-start.1
  88.1 1.2 copy-done.1
  89.3 29.8 %shard_map.85 = (bf16[4096,128]{1,0:T(8,128)(2,1)S(1)}, bf16[4096,256]{1,0:T(8,128)(2,1)}) custom-call(s32[2]{0:T(128)S(1)} %pad_add_fusion.scal_ref, bf16[4096,128]{1,0:T(8,128)(2,1)S(1)} %bitcast.16, bf16[4096,128]{1,0:T(8,128)(2,1)S(1)} %bitcast.17, bf16[4096,128]{1,0:T(8,128)(2,1)S(1)} %copy-done, bf16[4096,128]{1,0:T(8,128)(2,1)S(1)} %copy-done.1), custom_call_target="tpu_custom_call" | custom-call | tf_op jit(solution)/shard_map/pallas_call | solution.py:101
  119.1 0.0 reduce-scatter.2.cloned.1.call-update
  119.1 32.2 %all_to_all.54 = bf16[32,128,128]{2,1,0:T(8,128)(2,1)S(1)} all-to-all(bf16[32,128,128]{2,1,0:T(8,128)(2,1)S(1)} %bitcast.18), channel_id=1, replica_groups=mesh['depth'=8,'seq'=32] {'seq'}, dimensions={0} | all-to-all | bytes 2097152 | tf_op jit(solution)/shard_map/all_to_all | solution.py:138
  151.3 0.7 copy.11
  152.0 1.3 reshape.23
  153.2 9.9 %reduce-scatter.2.cloned.1.call-done = bf16[512,256]{1,0:T(8,128)(2,1)} async-done(((bf16[4096,256]{1,0:T(8,128)(2,1)}), bf16[512,256]{1,0:T(8,128)(2,1)}) %reduce-scatter.2.cloned.1.call-update) | async-done | bytes 262160 | tf_op jit(solution)/shard_map/reduce_scatter | solution.py:137
  163.1 1.7 fusion.2
Async XLA Ops:
  8.6 11.4 %copy-start.2 = (bf16[1,128,4096]{2,1,0:T(8,128)(2,1)S(1)}, bf16[1,128,4096]{2,1,0:T(8,128)(2,1)}, u32[]{:S(2)}) copy-start(bf16[1,128,4096]{2,1,0:T(8,128)(2,1)} %param.7) | copy-start | bytes 3145732
  10.0 25.9 %all-to-all-start = ((bf16[128,32,128]{2,0,1:T(8,128)(2,1)}), bf16[128,32,128]{2,0,1:T(8,128)(2,1)S(1)}, u32[]{:S(2)}, u32[]{:S(2)}) async-start(bf16[128,32,128]{2,0,1:T(8,128)(2,1)} %copy.9), calls=%async_computation | async-start | bytes 2097152 | tf_op jit(solution)/shard_map/all_to_all | solution.py:132
  19.2 36.5 %all-gather.3.cloned.1.call-start = ((), (), s32[]{:S(2)}) async-start(), calls=%async_computation.4 | async-start | bytes 1179648 | tf_op jit(solution)/shard_map/all_gather | solution.py:135
  20.2 20.4 %copy-start.3 = (s32[8]{0:T(128)S(1)}, s32[8]{0:T(128)}, u32[]{:S(2)}) copy-start(s32[8]{0:T(128)} %param.10) | copy-start | bytes 100
  20.3 20.4 %copy-start.4 = (s32[8]{0:T(128)S(1)}, s32[8]{0:T(128)}, u32[]{:S(2)}) copy-start(s32[8]{0:T(128)} %param.11) | copy-start | bytes 100
  35.9 50.9 %all-to-all-start.1 = ((bf16[128,32,128]{2,0,1:T(8,128)(2,1)}), bf16[128,32,128]{2,0,1:T(8,128)(2,1)S(1)}, u32[]{:S(2)}, u32[]{:S(2)}) async-start(bf16[128,32,128]{2,0,1:T(8,128)(2,1)} %copy.10), calls=%async_computation.1 | async-start | bytes 2097152 | tf_op jit(solution)/shard_map/all_to_all | solution.py:132
  39.9 47.0 %all-gather.5.cloned.1.call-start = ((), (), s32[]{:S(2)}) async-start(), calls=%async_computation.5 | async-start | bytes 1179648 | tf_op jit(solution)/shard_map/all_gather | solution.py:135
  40.6 122.5 %reduce-scatter.2.cloned.1.call-start = ((), (), s32[]{:S(2)}) async-start(), calls=%async_computation.6 | async-start | bytes 2359296 | tf_op jit(solution)/shard_map/reduce_scatter | solution.py:137
  86.9 1.2 copy-start
  88.1 1.2 copy-start.1
Sparse Core Ops, SparseCore 0:
  21.9 33.7 all-gather.2
  57.6 29.1 all-gather.4
  119.2 43.8 reduce-scatter.1

commit v2 on v1

v2 whole, which is shorter than its diff:
```python
import functools
import math

import jax
import jax.numpy as jnp
from jax import lax
from jax.experimental import pallas as pl
from jax.experimental.pallas import tpu as pltpu
from jax.sharding import PartitionSpec as P

HD = 128
WIN = 1024
BLK = 128
SIDE = 4
PEERS = SIDE * SIDE
RING = 8
SHARD = 512
TOTAL = 4096
PAD = TOTAL + WIN + BLK
SPAN = WIN + 3 * BLK + 16
TAIL = 1536
NEG = -1e30
SCALE = 1.0 / math.sqrt(HD)
SCALE2 = SCALE * math.log2(math.e)
F32 = jnp.float32
BF16 = jnp.bfloat16
MESH = pl.DeviceIdType.MESH

BLOCKS = (
    (0, 256, "a", "low"),
    (256, 384, "ab", "low"),
    (640, 384, "ab", "low"),
    (1024, 144, "ab", "high"),
    (1168, 112, "b", None),
    (1280, 144, "b", "high"),
)
COLS = {"a": (0, BLK), "b": (BLK, BLK), "ab": (0, 2 * BLK)}
MOVES = (
    (0, 1), (1, 0), (0, 3), (3, 0), (1, 1), (3, 3), (1, 3), (3, 1),
    (0, 2), (2, 0), (2, 1), (1, 2), (2, 3), (3, 2), (2, 2),
)
FLOWS = ((0, 1, 4), (1, -1, 4), (0, -1, 3), (1, 1, 3))


def dot_t(a, b):
    return lax.dot_general(a, b, (((1,), (1,)), ((), ())), preferred_element_type=F32)


def dot(a, b):
    return jnp.dot(a, b, preferred_element_type=F32)


def fused_kernel(
    off_ref, win_ref, q_in, g_in, k_in, v_in,
    dq_out, dk_out, dv_out,
    qg, kv, kt, acc, s_scr, dp_scr, ds_scr, dqs, sib_out, sib_in, ring_out, ring_in,
    x_send, x_recv, own_sem, ag_send, ag_recv, sb_send, sb_recv, dq_send, dq_recv, dq_own,
    ss_send, ss_recv, rs_send, rs_recv,
):
    depth = lax.axis_index("depth")
    seq = lax.axis_index("seq")
    core = depth % 2
    z_lo = seq % 2
    col = seq // 2
    x = col // SIDE
    y = col % SIDE
    z = (depth // 2) * 2 + z_lo

    def at_xy(dx, dy):
        return (depth, (((x + dx) % SIDE) * SIDE + (y + dy) % SIDE) * 2 + z_lo)

    def at_z(to):
        return ((to // 2) * 2 + core, col * 2 + to % 2)

    up = at_z((z + 1) % RING)
    down = at_z((z + RING - 1) % RING)
    sibling = (depth + 1 - 2 * core, seq)

    barrier = pltpu.get_barrier_semaphore()
    partners = [at_xy(*m) for m in MOVES] + [up, down, sibling]
    for dev in partners:
        pl.semaphore_signal(barrier, inc=1, device_id=dev, device_id_type=MESH)
    pl.semaphore_wait(barrier, len(partners))

    def remote(src, dst, send, recv, dev):
        return pltpu.make_async_remote_copy(
            src_ref=src, dst_ref=dst, send_sem=send, recv_sem=recv, device_id=dev, device_id_type=MESH
        )

    def slot(t, origin, side):
        row = pl.multiple_of(WIN + ((origin // 2) * 2 + side) * SHARD, SHARD)
        return kv.at[t, origin % 2, pl.ds(row, SHARD), :]

    own_kv = (k_in, v_in)
    ring = {}
    sent = []
    for f, (t, way, hops) in enumerate(FLOWS):
        c = remote(own_kv[t], slot(t, z, core), ag_send.at[f, 0], ag_recv.at[f, 0], up if way > 0 else down)
        c.start()
        ring[f, 0] = c
    side = {}
    for t in range(2):
        c = remote(own_kv[t], slot(t, z, core), sb_send.at[4, t], sb_recv.at[4, t], sibling)
        c.start()
        side[4, t] = c
    local = []
    for t in range(2):
        c = pltpu.make_async_copy(own_kv[t], slot(t, z, core), own_sem.at[0, t])
        c.start()
        local.append(c)
    mine = pl.multiple_of(col * BLK, BLK)
    exchange = []
    for h in range(2):
        for t, src in enumerate((q_in, g_in)):
            c = pltpu.make_async_copy(
                src.at[:, pl.ds(pl.multiple_of((col * 2 + h) * HD, HD), HD)],
                qg.at[h, t, pl.ds(mine, BLK), :],
                own_sem.at[1 + h, t],
            )
            c.start()
            local.append(c)
            for i, (dx, dy) in enumerate(MOVES):
                to = ((x + dx) % SIDE) * SIDE + (y + dy) % SIDE
                c = remote(
                    src.at[:, pl.ds(pl.multiple_of((to * 2 + h) * HD, HD), HD)],
                    qg.at[h, t, pl.ds(mine, BLK), :],
                    x_send.at[h, t, i],
                    x_recv.at[h, t, i],
                    at_xy(dx, dy),
                )
                c.start()
                exchange.append(c)

    for h in range(2):
        for t in range(2):
            kv[t, h, pl.ds(0, WIN), :] = jnp.zeros((WIN, HD), BF16)
            kv[t, h, pl.ds(WIN + TOTAL, BLK), :] = jnp.zeros((BLK, HD), BF16)
    acc[...] = jnp.zeros_like(acc)
    ds_scr[...] = jnp.zeros_like(ds_scr)

    for hop in range(4):
        for f, (t, way, hops) in enumerate(FLOWS):
            if hop >= hops:
                continue
            ring[f, hop].wait_recv()
            origin = (z + 2 * RING - way * (hop + 1)) % RING
            here = slot(t, origin, core)
            if hop + 1 < hops:
                c = remote(
                    here, here, ag_send.at[f, hop + 1], ag_recv.at[f, hop + 1], up if way > 0 else down
                )
                c.start()
                ring[f, hop + 1] = c
            c = remote(here, here, sb_send.at[f, hop], sb_recv.at[f, hop], sibling)
            c.start()
            side[f, hop] = c
    for c in side.values():
        c.wait_recv()
    for c in local:
        c.wait()
    for c in exchange:
        c.wait_recv()

    for h in range(2):
        def turn(i, carry, h=h):
            row = pl.multiple_of(i * 256, 256)
            kt[h, :, pl.ds(row, 256)] = kv[0, h, pl.ds(row, 256), :].T
            return carry

        lax.fori_loop(0, PAD // 256, turn, 0)
        kt[h, :, pl.ds(PAD - BLK, BLK)] = jnp.zeros((HD, BLK), BF16)

    shift = off_ref[depth]
    span = win_ref[depth]
    lane = lax.broadcasted_iota(jnp.int32, (1, 2 * BLK), 1)
    place = lane + jnp.where(lane >= BLK, BLK, 0)
    last = place + WIN + shift

    def tile(n, carry):
        h = n // 8
        u = n % 8
        base = pl.multiple_of((4 * u + z_lo) * BLK, BLK)
        low = jnp.maximum(last - span, WIN - 1 - base)
        high = jnp.minimum(last, TOTAL + WIN - 1 - base)
        rows_q = pl.multiple_of(u * 2 * BLK, 2 * BLK)
        q = qg[h, 0, pl.ds(rows_q, 2 * BLK), :]
        g = qg[h, 1, pl.ds(rows_q, 2 * BLK), :]

        def join(part, value, halves, op):
            c0, n0 = COLS[halves]
            if halves == "ab":
                return op(part, value)
            if halves == "a":
                return jnp.concatenate([op(part[:, :BLK], value), part[:, BLK:]], axis=1)
            return jnp.concatenate([part[:, :BLK], op(part[:, BLK:], value)], axis=1)

        top = jnp.full((1, 2 * BLK), NEG, F32)
        for k0, rows, halves, bound in BLOCKS:
            c0, cn = COLS[halves]
            at = pl.multiple_of(base + k0, 16)
            s = dot_t(kv[0, h, pl.ds(at, rows), :], q[c0 : c0 + cn])
            if bound is not None:
                key = lax.broadcasted_iota(jnp.int32, (rows, cn), 0)
                if bound == "low":
                    keep = key > low[:, c0 : c0 + cn] - k0
                else:
                    keep = key <= high[:, c0 : c0 + cn] - k0
                s = jnp.where(keep, s, NEG)
            s_scr[pl.ds(k0, rows), pl.ds(c0, cn)] = s
            top = join(top, jnp.max(s, axis=0, keepdims=True), halves, jnp.maximum)
        top = top * SCALE2
        sum_e = jnp.zeros((1, 2 * BLK), F32)
        sum_d = jnp.zeros((1, 2 * BLK), F32)
        for k0, rows, halves, bound in BLOCKS:
            c0, cn = COLS[halves]
            at = pl.multiple_of(base + k0, 16)
            dp = dot_t(kv[1, h, pl.ds(at, rows), :], g[c0 : c0 + cn])
            e = jnp.exp2(s_scr[pl.ds(k0, rows), pl.ds(c0, cn)] * SCALE2 - top[:, c0 : c0 + cn])
            sum_e = join(sum_e, jnp.sum(e, axis=0, keepdims=True), halves, jnp.add)
            sum_d = join(sum_d, jnp.sum(e * dp, axis=0, keepdims=True), halves, jnp.add)
            s_scr[pl.ds(k0, rows), pl.ds(c0, cn)] = e
            dp_scr[pl.ds(k0, rows), pl.ds(c0, cn)] = dp
        inv = 1.0 / sum_e
        rowdot = sum_d * inv
        for k0, rows, halves, bound in BLOCKS:
            c0, cn = COLS[halves]
            at = pl.multiple_of(base + k0, 16)
            p = s_scr[pl.ds(k0, rows), pl.ds(c0, cn)] * inv[:, c0 : c0 + cn]
            ds = p * (dp_scr[pl.ds(k0, rows), pl.ds(c0, cn)] - rowdot[:, c0 : c0 + cn])
            ds = ds.astype(BF16)
            ds_scr[pl.ds(k0, rows), pl.ds(c0, cn)] = ds
            acc[1, h, pl.ds(at, rows), :] += dot(p.astype(BF16), g[c0 : c0 + cn])
            acc[0, h, pl.ds(at, rows), :] += dot(ds, q[c0 : c0 + cn])
        dqt = dot(kt[h, :, pl.ds(base, TAIL)], ds_scr[...])
        dqs[h, pl.ds(rows_q, 2 * BLK), :] = (dqt.T * SCALE).astype(BF16)

        for half in range(2):
            to = 2 * u + half
            src = dqs.at[h, pl.ds(pl.multiple_of(to * BLK, BLK), BLK), :]
            dst = dq_out.at[:, pl.ds(pl.multiple_of((col * 2 + h) * HD, HD), HD)]

            @pl.when(to != col)
            def _():
                remote(src, dst, dq_send.at[h, to], dq_recv.at[h, col], (depth, to * 2 + z_lo)).start()

            @pl.when(to == col)
            def _():
                pltpu.make_async_copy(src, dst, dq_own.at[h]).start()

        return carry

    lax.fori_loop(0, 16, tile, 0)

    scale_of = (SCALE, 1.0)

    def partial(t, target, side):
        row = pl.multiple_of(WIN + ((target // 2) * 2 + side) * SHARD, SHARD)
        value = acc[t, target % 2, pl.ds(row, SHARD), :]
        return value * SCALE if t == 0 else value

    swaps = {}
    for away in (4, 3, 5, 2, 6, 1, 7, 0):
        target = (z + away) % RING
        for t in range(2):
            sib_out[target, t] = partial(t, target, 1 - core).astype(BF16)
        c = remote(
            sib_out.at[target], sib_in.at[target], ss_send.at[away], ss_recv.at[away], sibling
        )
        c.start()
        swaps[away] = c

    def chip_sum(t, target):
        return partial(t, target, core) + sib_in[target, t].astype(F32)

    seen = set()
    hop_out = {}
    for left in (4, 3, 2, 1):
        for f, (t, way, hops) in enumerate(FLOWS):
            if left > hops:
                continue
            away = (way * left) % RING
            if away not in seen:
                seen.add(away)
                swaps[away].wait_recv()
            target = (z + away) % RING
            value = chip_sum(t, target)
            if left < hops:
                hop_out[f, left + 1].wait_recv()
                value += ring_in[f, left].astype(F32)
            ring_out[f, left - 1] = value.astype(BF16)
            c = remote(
                ring_out.at[f, left - 1], ring_in.at[f, left - 1],
                rs_send.at[f, left - 1], rs_recv.at[f, left - 1], up if way > 0 else down,
            )
            c.start()
            hop_out[f, left] = c
    swaps[0].wait_recv()
    for t, dst in enumerate((dk_out, dv_out)):
        value = chip_sum(t, z)
        for f, (tf, way, hops) in enumerate(FLOWS):
            if tf == t:
                hop_out[f, 1].wait_recv()
                value += ring_in[f, 0].astype(F32)
        dst[...] = value.astype(BF16)

    for h in range(2):
        dst = dq_out.at[:, pl.ds(pl.multiple_of((col * 2 + h) * HD, HD), HD)]
        pltpu.make_async_copy(dqs.at[h, pl.ds(mine, BLK), :], dst, dq_own.at[h]).wait()
        for dx, dy in MOVES:
            to = ((x + dx) % SIDE) * SIDE + (y + dy) % SIDE
            src = dqs.at[h, pl.ds(pl.multiple_of(to * BLK, BLK), BLK), :]
            into = dq_out.at[:, pl.ds(pl.multiple_of((to * 2 + h) * HD, HD), HD)]
            remote(src, into, dq_send.at[h, to], dq_recv.at[h, to], at_xy(dx, dy)).wait()
    for c in list(ring.values()) + list(side.values()) + exchange + list(swaps.values()) + list(hop_out.values()):
        c.wait_send()


def on_device(queries, grad_out, key_states, value_states, offsets, windows):
    rows, width = queries.shape[1:]
    anywhere = pl.BlockSpec(memory_space=pl.ANY)
    vmem = pl.BlockSpec(memory_space=pltpu.VMEM)
    smem = pl.BlockSpec(memory_space=pltpu.SMEM)
    dma = pltpu.SemaphoreType.DMA
    dq, dk, dv = pl.pallas_call(
        fused_kernel,
        out_shape=(
            jax.ShapeDtypeStruct((rows, width), BF16),
            jax.ShapeDtypeStruct(key_states.shape, BF16),
            jax.ShapeDtypeStruct(key_states.shape, BF16),
        ),
        in_specs=[smem, smem] + [anywhere] * 4,
        out_specs=(anywhere, vmem, vmem),
        scratch_shapes=[
            pltpu.VMEM((2, 2, PEERS * BLK, HD), BF16),
            pltpu.VMEM((2, 2, PAD, HD), BF16),
            pltpu.VMEM((2, HD, PAD), BF16),
            pltpu.VMEM((2, 2, PAD, HD), F32),
            pltpu.VMEM((SPAN, 2 * BLK), F32),
            pltpu.VMEM((SPAN, 2 * BLK), F32),
            pltpu.VMEM((TAIL, 2 * BLK), BF16),
            pltpu.VMEM((2, PEERS * BLK, HD), BF16),
            pltpu.VMEM((RING, 2, SHARD, HD), BF16),
            pltpu.VMEM((RING, 2, SHARD, HD), BF16),
            pltpu.VMEM((4, 4, SHARD, HD), BF16),
            pltpu.VMEM((4, 4, SHARD, HD), BF16),
            dma((2, 2, 15)), dma((2, 2, 15)), dma((3, 2)),
            dma((4, 4)), dma((4, 4)), dma((5, 4)), dma((5, 4)),
            dma((2, 16)), dma((2, 16)), dma((2,)),
            dma((8,)), dma((8,)), dma((4, 4)), dma((4, 4)),
        ],
        compiler_params=pltpu.CompilerParams(
            collective_id=0, has_side_effects=True, vmem_limit_bytes=56 << 20
        ),
    )(
        offsets, windows, queries.reshape(rows, width), grad_out.reshape(rows, width),
        key_states, value_states,
    )
    return dq.reshape(1, rows, width), dk, dv


def solution(mesh):
    in_specs = (
        P("depth", "seq", None),
        P("depth", "seq", None),
        P("depth", "seq"),
        P("depth", "seq"),
        P(),
        P(),
    )
    out_specs = (P("depth", "seq", None), P("depth", "seq"), P("depth", "seq"))
    return jax.shard_map(
        on_device, mesh=mesh, in_specs=in_specs, out_specs=out_specs, check_vma=False
    )
```

time: 174 us -> 96.8 us (0.56); the launches traced: 171 us -> 96.7 us
  waiting for transfers between devices: 69.7 us -> 0 us
  Pallas kernels: 29.8 us -> 92.1 us
  blocking collectives: 32.2 us -> 0 us
  starting transfers between devices: 13.3 us -> 0 us
  between operations: 13.8 us -> 0.65 us
  local copies, waits for them, and re-layouts: 10.6 us -> 3.93 us
  other arithmetic: 2 us -> 0 us
    pallas_call x1, Pallas kernels: 29.8 us -> 92.1 us  [on_device(): pl.pallas_call(fused_kernel, out_shape=(jax.ShapeDtypeStruct((rows, width...]
    all_gather x2 -> x0, waiting for transfers between devices: 44.2 us -> none  [on_device(): lax.all_gather(a, 'depth', axis=0, tiled=True)]
    all_to_all x1 -> x0, blocking collectives: 32.2 us -> none  [on_device(): back = lax.all_to_all(dq, 'seq', split_axis=0, concat_axis=1, tiled=True)]
    all_to_all x2 -> x0, waiting for transfers between devices: 14.3 us -> none  [on_device(): lax.all_to_all(a.reshape(tok_rows, model_width), 'seq', split_axis=1, con...]
    all_to_all x2 -> x0, starting transfers between devices: 13.2 us -> none  [on_device(): lax.all_to_all(a.reshape(tok_rows, model_width), 'seq', split_axis=1, con...]
    reduce_scatter x1 -> x0, waiting for transfers between devices: 9.9 us -> none  [on_device(): summed = lax.psum_scatter(dkv, 'depth', scatter_dimension=0, tiled=True)]
    all_to_all x3 -> x0, local copies, waits for them, and re-layouts: 3.44 us -> none  [the longest x2 2.76 us: on_device(): lax.all_to_all(a.reshape(tok_rows, model_width), 'seq', split_axis=1, con...]
    unnamed x12 -> x7, local copies, waits for them, and re-layouts: 4.16 us -> 3.93 us
  transfers between devices with their start and end apart: 5 -> 0, of which waited for: 4 -> 0; matrix products, arithmetic and copies ran while one was open for 3% -> 0% of each run, Pallas kernels for 0% -> 0%
where the time goes in v2:
time: 96.8 us; the launch traced here: 96.7 us
  Pallas kernels  92.1 us (95%)
  local copies, waits for them, and re-layouts  3.93 us (4%)
    pallas_call x1, Pallas kernels, on_device(): pl.pallas_call(fused_kernel, out_shape=(jax.ShapeDtypeStruct((rows, width...  92.1 us
    unnamed x7, local copies, waits for them, and re-layouts  3.93 us

profile of v2, /device:TPU:1, one launch (start us, length us, event | category | flops | bytes accessed | tf_op | source)
XLA Modules:
  0.0 96.7 jit_solution(2369190122913775879)
XLA Ops:
  0.6 92.1 %shard_map.85 = (bf16[128,4096]{1,0:T(8,128)(2,1)}, bf16[512,128]{1,0:T(8,128)(2,1)}, bf16[512,128]{1,0:T(8,128)(2,1)}) custom-call(s32[8]{0:T(128)} %off_ref.1, s32[8]{0:T(128)} %win_ref.1, bf16[128,4096]{1,0:T(8,128)(2,1)} %bitcast.3, bf16[128,4096]{1,0:T(8,128)(2,1)} %bitcast.4, bf16[512,128]{1,0:T(8,128)(2,1)} %k_in.1, bf16[512,128]{1,0:T(8,128)(2,1)} %v_in.1), custom_call_target="tpu_custom_call" | custom-call | tf_op jit(solution)/shard_map/pallas_call | solution.py:324
  92.7 0.0 copy-start.1
  92.8 2.3 %copy.12 = bf16[1,128,4096]{2,1,0:T(8,128)(2,1)} copy(bf16[1,128,4096]{2,1,0:T(8,128)(2,1)} %bitcast.5) | data formatting | bytes 2097152
  95.1 0.0 copy-done.1
  95.1 0.0 copy-start
  95.1 0.7 copy.13
  95.7 0.3 copy-done
  96.0 0.7 copy.14
Async XLA Ops:
  92.7 2.3 %copy-start.1 = (bf16[512,128]{1,0:T(8,128)(2,1)S(1)}, bf16[512,128]{1,0:T(8,128)(2,1)}, u32[]{:S(2)}) copy-start(bf16[512,128]{1,0:T(8,128)(2,1)} %get-tuple-element.13) | copy-start | bytes 393220
  95.1 1.0 copy-start

commit v3 on v2

--- a/solution.py
+++ b/solution.py
@@ -40,6 +40,7 @@
     (0, 2), (2, 0), (2, 1), (1, 2), (2, 3), (3, 2), (2, 2),
 )
 FLOWS = ((0, 1, 4), (1, -1, 4), (0, -1, 3), (1, 1, 3))
+SUM_HOPS = {-1: 4, 1: 3}
 
 
 def dot_t(a, b):
@@ -92,83 +93,188 @@
         return kv.at[t, origin % 2, pl.ds(row, SHARD), :]
 
     own_kv = (k_in, v_in)
-    ring = {}
-    sent = []
-    for f, (t, way, hops) in enumerate(FLOWS):
-        c = remote(own_kv[t], slot(t, z, core), ag_send.at[f, 0], ag_recv.at[f, 0], up if way > 0 else down)
-        c.start()
-        ring[f, 0] = c
-    side = {}
-    for t in range(2):
-        c = remote(own_kv[t], slot(t, z, core), sb_send.at[4, t], sb_recv.at[4, t], sibling)
-        c.start()
-        side[4, t] = c
-    local = []
-    for t in range(2):
-        c = pltpu.make_async_copy(own_kv[t], slot(t, z, core), own_sem.at[0, t])
-        c.start()
-        local.append(c)
+
+    def along(way):
+        return up if way > 0 else down
+
+    def ring_copy(f, hop, src, dst):
+        return remote(src, dst, ag_send.at[f, hop], ag_recv.at[f, hop], along(FLOWS[f][1]))
+
+    def side_copy(f, hop, src, dst):
+        return remote(src, dst, sb_send.at[f, hop], sb_recv.at[f, hop], sibling)
+
+    def send_own():
+        for f, (t, way, hops) in enumerate(FLOWS):
+            ring_copy(f, 0, own_kv[t], slot(t, z, core)).start()
+        for t in range(2):
+            side_copy(4, t, own_kv[t], slot(t, z, core)).start()
+
+    def turn(origin, side):
+        row = pl.multiple_of(WIN + ((origin // 2) * 2 + side) * SHARD, SHARD)
+        kt[origin % 2, :, pl.ds(row, SHARD)] = kv[0, origin % 2, pl.ds(row, SHARD), :].T
+
+    def ring_step(h, r):
+        far = (z + h) % 2
+        away = 2 * r - far
+        for f, (t, way, hops) in enumerate(FLOWS):
+            origin = (z + 2 * RING - way * away) % RING
+            here = slot(t, origin, core)
+
+            @pl.when(away <= hops)
+            def _():
+                ring_copy(f, away - 1, here, here).wait_recv()
+
+                @pl.when(away < hops)
+                def _():
+                    ring_copy(f, away, here, here).start()
+
+                side_copy(f, away - 1, here, here).start()
+
+        for f, (t, way, hops) in enumerate(FLOWS):
+            if t == 0:
+                origin = (z + 2 * RING - way * away) % RING
+
+                @pl.when(away <= hops)
+                def _():
+                    turn(origin, core)
+
+    def side_wait(h):
+        far = (z + h) % 2
+
+        @pl.when(far == 0)
+        def _():
+            for t in range(2):
+                there = slot(t, z, 1 - core)
+                side_copy(4, t, there, there).wait_recv()
+            turn(z, 1 - core)
+
+        for r in (1, 2):
+            away = 2 * r - far
+            for f, (t, way, hops) in enumerate(FLOWS):
+                origin = (z + 2 * RING - way * away) % RING
+                there = slot(t, origin, 1 - core)
+
+                @pl.when(away <= hops)
+                def _():
+                    side_copy(f, away - 1, there, there).wait_recv()
+                    if t == 0:
+                        turn(origin, 1 - core)
+
     mine = pl.multiple_of(col * BLK, BLK)
-    exchange = []
-    for h in range(2):
-        for t, src in enumerate((q_in, g_in)):
-            c = pltpu.make_async_copy(
-                src.at[:, pl.ds(pl.multiple_of((col * 2 + h) * HD, HD), HD)],
-                qg.at[h, t, pl.ds(mine, BLK), :],
-                own_sem.at[1 + h, t],
-            )
-            c.start()
-            local.append(c)
-            for i, (dx, dy) in enumerate(MOVES):
+
+    def cross(h):
+        for i, (dx, dy) in enumerate(MOVES):
+            for t, src in enumerate((q_in, g_in)):
                 to = ((x + dx) % SIDE) * SIDE + (y + dy) % SIDE
-                c = remote(
+                yield remote(
                     src.at[:, pl.ds(pl.multiple_of((to * 2 + h) * HD, HD), HD)],
                     qg.at[h, t, pl.ds(mine, BLK), :],
                     x_send.at[h, t, i],
                     x_recv.at[h, t, i],
                     at_xy(dx, dy),
                 )
-                c.start()
-                exchange.append(c)
-
+
+    local = []
+    for t in range(2):
+        local.append(pltpu.make_async_copy(own_kv[t], slot(t, z, core), own_sem.at[0, t]))
+    for h in range(2):
+        for t, src in enumerate((q_in, g_in)):
+            local.append(
+                pltpu.make_async_copy(
+                    src.at[:, pl.ds(pl.multiple_of((col * 2 + h) * HD, HD), HD)],
+                    qg.at[h, t, pl.ds(mine, BLK), :],
+                    own_sem.at[1 + h, t],
+                )
+            )
+
+    @pl.when(z_lo == 1)
+    def _():
+        send_own()
+
+    for c in cross(1):
+        c.start()
+    for c in local:
+        c.start()
     for h in range(2):
         for t in range(2):
             kv[t, h, pl.ds(0, WIN), :] = jnp.zeros((WIN, HD), BF16)
             kv[t, h, pl.ds(WIN + TOTAL, BLK), :] = jnp.zeros((BLK, HD), BF16)
+        kt[h, :, pl.ds(0, WIN)] = jnp.zeros((HD, WIN), BF16)
+        kt[h, :, pl.ds(WIN + TOTAL, BLK)] = jnp.zeros((HD, BLK), BF16)
     acc[...] = jnp.zeros_like(acc)
     ds_scr[...] = jnp.zeros_like(ds_scr)
-
-    for hop in range(4):
-        for f, (t, way, hops) in enumerate(FLOWS):
-            if hop >= hops:
-                continue
-            ring[f, hop].wait_recv()
-            origin = (z + 2 * RING - way * (hop + 1)) % RING
-            here = slot(t, origin, core)
-            if hop + 1 < hops:
-                c = remote(
-                    here, here, ag_send.at[f, hop + 1], ag_recv.at[f, hop + 1], up if way > 0 else down
-                )
-                c.start()
-                ring[f, hop + 1] = c
-            c = remote(here, here, sb_send.at[f, hop], sb_recv.at[f, hop], sibling)
-            c.start()
-            side[f, hop] = c
-    for c in side.values():
-        c.wait_recv()
     for c in local:
         c.wait()
-    for c in exchange:
+
+    ring_step(1, 1)
+
+    @pl.when(z_lo == 0)
+    def _():
+        send_own()
+
+    turn(z, core)
+
+    @pl.when(z_lo == 1)
+    def _():
+        ring_step(0, 1)
+
+    for c in cross(1):
+        c.wait_send()
+    for c in cross(0):
+        c.start()
+    ring_step(1, 2)
+
+    @pl.when(z_lo == 0)
+    def _():
+        ring_step(0, 1)
+
+    side_wait(1)
+    for c in cross(1):
         c.wait_recv()
 
-    for h in range(2):
-        def turn(i, carry, h=h):
-            row = pl.multiple_of(i * 256, 256)
-            kt[h, :, pl.ds(row, 256)] = kv[0, h, pl.ds(row, 256), :].T
-            return carry
-
-        lax.fori_loop(0, PAD // 256, turn, 0)
-        kt[h, :, pl.ds(PAD - BLK, BLK)] = jnp.zeros((HD, BLK), BF16)
+    quarter = depth // 2
+
+    def partial(t, target, side):
+        row = pl.multiple_of(WIN + ((target // 2) * 2 + side) * SHARD, SHARD)
+        value = acc[t, target % 2, pl.ds(row, SHARD), :]
+        return value * SCALE if t == 0 else value
+
+    def swap_copy(target):
+        return remote(
+            sib_out.at[target], sib_in.at[target], ss_send.at[target], ss_recv.at[target], sibling
+        )
+
+    def swap(h, ahead):
+        target = ((quarter + ahead) % 4) * 2 + h
+        for t in range(2):
+            sib_out[target, t] = partial(t, target, 1 - core).astype(BF16)
+        swap_copy(target).start()
+
+    def chip_sum(t, target):
+        return partial(t, target, core) + sib_in[target, t].astype(F32)
+
+    def sum_copy(t, way, left):
+        f = 2 * t + (1 if way > 0 else 0)
+        return remote(
+            ring_out.at[f, left - 1], ring_in.at[f, left - 1],
+            rs_send.at[f, left - 1], rs_recv.at[f, left - 1], along(way),
+        )
+
+    def sum_round(h, far_round, way, near, add):
+        left = (4 if far_round else 2) - near
+
+        @pl.when((z + h) % 2 == near)
+        def _():
+            target = (z + RING + way * left) % RING
+            swap_copy(target).wait_recv()
+            for t in range(2):
+                f = 2 * t + (1 if way > 0 else 0)
+                value = chip_sum(t, target)
+                if add:
+                    sum_copy(t, way, left + 1).wait_recv()
+                    value += ring_in[f, left].astype(F32)
+                ring_out[f, left - 1] = value.astype(BF16)
+                sum_copy(t, way, left).start()
 
     shift = off_ref[depth]
     span = win_ref[depth]
@@ -176,9 +282,70 @@
     place = lane + jnp.where(lane >= BLK, BLK, 0)
     last = place + WIN + shift
 
+    def steps(n):
+        def step(k):
+            return pl.when(n == k)
+
+        @pl.when(n == 5 - 2 * z_lo)
+        def _():
+            ring_step(0, 2)
+
+        @step(5)
+        def _():
+            swap(1, 2)
+
+        @step(7)
+        def _():
+            swap(1, 3)
+
+        @step(8)
+        def _():
+            swap(1, 0)
+            swap(1, 1)
+            side_wait(0)
+            for c in cross(0):
+                c.wait_recv()
+
+        @step(9)
+        def _():
+            sum_round(1, True, -1, 0, False)
+            sum_round(1, True, 1, 1, False)
+
+        @step(11)
+        def _():
+            sum_round(1, True, -1, 1, True)
+
+        @step(12 + z_lo)
+        def _():
+            swap(0, 2)
+
+        @step(12)
+        def _():
+            sum_round(1, False, 1, 0, True)
+
+        @step(13)
+        def _():
+            sum_round(1, False, -1, 0, True)
+            sum_round(0, True, -1, 0, False)
+
+        @step(14 + z_lo)
+        def _():
+            swap(0, 3)
+
+        @step(14)
+        def _():
+            sum_round(0, True, 1, 1, False)
+
+        @step(15)
+        def _():
+            sum_round(1, False, 1, 1, True)
+            sum_round(1, False, -1, 1, True)
+            sum_round(0, True, -1, 1, True)
+
     def tile(n, carry):
-        h = n // 8
-        u = n % 8
+        steps(n)
+        h = 1 - n // 8
+        u = (2 * quarter + 4 - z_lo + n) % 8
         base = pl.multiple_of((4 * u + z_lo) * BLK, BLK)
         low = jnp.maximum(last - span, WIN - 1 - base)
         high = jnp.minimum(last, TOTAL + WIN - 1 - base)
@@ -251,56 +418,18 @@
 
     lax.fori_loop(0, 16, tile, 0)
 
-    scale_of = (SCALE, 1.0)
-
-    def partial(t, target, side):
-        row = pl.multiple_of(WIN + ((target // 2) * 2 + side) * SHARD, SHARD)
-        value = acc[t, target % 2, pl.ds(row, SHARD), :]
-        return value * SCALE if t == 0 else value
-
-    swaps = {}
-    for away in (4, 3, 5, 2, 6, 1, 7, 0):
-        target = (z + away) % RING
-        for t in range(2):
-            sib_out[target, t] = partial(t, target, 1 - core).astype(BF16)
-        c = remote(
-            sib_out.at[target], sib_in.at[target], ss_send.at[away], ss_recv.at[away], sibling
-        )
-        c.start()
-        swaps[away] = c
-
-    def chip_sum(t, target):
-        return partial(t, target, core) + sib_in[target, t].astype(F32)
-
-    seen = set()
-    hop_out = {}
-    for left in (4, 3, 2, 1):
-        for f, (t, way, hops) in enumerate(FLOWS):
-            if left > hops:
-                continue
-            away = (way * left) % RING
-            if away not in seen:
-                seen.add(away)
-                swaps[away].wait_recv()
-            target = (z + away) % RING
-            value = chip_sum(t, target)
-            if left < hops:
-                hop_out[f, left + 1].wait_recv()
-                value += ring_in[f, left].astype(F32)
-            ring_out[f, left - 1] = value.astype(BF16)
-            c = remote(
-                ring_out.at[f, left - 1], ring_in.at[f, left - 1],
-                rs_send.at[f, left - 1], rs_recv.at[f, left - 1], up if way > 0 else down,
-            )
-            c.start()
-            hop_out[f, left] = c
-    swaps[0].wait_recv()
+    swap(0, 1)
+    swap(0, 0)
+    sum_round(0, False, -1, 0, True)
+    sum_round(0, False, 1, 0, True)
+    sum_round(0, False, -1, 1, True)
+    sum_round(0, False, 1, 1, True)
+    swap_copy(z).wait_recv()
     for t, dst in enumerate((dk_out, dv_out)):
         value = chip_sum(t, z)
-        for f, (tf, way, hops) in enumerate(FLOWS):
-            if tf == t:
-                hop_out[f, 1].wait_recv()
-                value += ring_in[f, 0].astype(F32)
+        for way in (-1, 1):
+            sum_copy(t, way, 1).wait_recv()
+            value += ring_in[2 * t + (1 if way > 0 else 0), 0].astype(F32)
         dst[...] = value.astype(BF16)
 
     for h in range(2):
@@ -311,8 +440,22 @@
             src = dqs.at[h, pl.ds(pl.multiple_of(to * BLK, BLK), BLK), :]
             into = dq_out.at[:, pl.ds(pl.multiple_of((to * 2 + h) * HD, HD), HD)]
             remote(src, into, dq_send.at[h, to], dq_recv.at[h, to], at_xy(dx, dy)).wait()
-    for c in list(ring.values()) + list(side.values()) + exchange + list(swaps.values()) + list(hop_out.values()):
+    for f, (t, way, hops) in enumerate(FLOWS):
+        for hop in range(hops):
+            here = slot(t, z, core)
+            ring_copy(f, hop, here, here).wait_send()
+            side_copy(f, hop, here, here).wait_send()
+    for t in range(2):
+        here = slot(t, z, core)
+        side_copy(4, t, here, here).wait_send()
+    for c in cross(0):
         c.wait_send()
+    for target in range(RING):
+        swap_copy(target).wait_send()
+    for way, hops in SUM_HOPS.items():
+        for t in range(2):
+            for left in range(1, hops + 1):
+                sum_copy(t, way, left).wait_send()
 
 
 def on_device(queries, grad_out, key_states, value_states, offsets, windows):

time: 96.8 us -> 98.1 us (1.013)
  Pallas kernels: 92.1 us -> 93.3 us
    pallas_call x1, Pallas kernels: 92.1 us -> 93.3 us  [on_device(): pl.pallas_call(fused_kernel, out_shape=(jax.ShapeDtypeStruct((rows, width...]
where the time goes in v3:
time: 98.1 us; the launch traced here: 97.9 us
  Pallas kernels  93.3 us (95%)
  local copies, waits for them, and re-layouts  3.93 us (4%)
    pallas_call x1, Pallas kernels, on_device(): pl.pallas_call(fused_kernel, out_shape=(jax.ShapeDtypeStruct((rows, width...  93.3 us
    unnamed x7, local copies, waits for them, and re-layouts  3.93 us

profile of v3, /device:TPU:1, one launch (start us, length us, event | category | flops | bytes accessed | tf_op | source)
XLA Modules:
  0.0 97.9 jit_solution(17863851659048197287)
XLA Ops:
  0.6 93.3 %shard_map.85 = (bf16[128,4096]{1,0:T(8,128)(2,1)}, bf16[512,128]{1,0:T(8,128)(2,1)}, bf16[512,128]{1,0:T(8,128)(2,1)}) custom-call(s32[8]{0:T(128)} %off_ref.1, s32[8]{0:T(128)} %win_ref.1, bf16[128,4096]{1,0:T(8,128)(2,1)} %bitcast.3, bf16[128,4096]{1,0:T(8,128)(2,1)} %bitcast.4, bf16[512,128]{1,0:T(8,128)(2,1)} %k_in.1, bf16[512,128]{1,0:T(8,128)(2,1)} %v_in.1), custom_call_target="tpu_custom_call" | custom-call | tf_op jit(solution)/shard_map/pallas_call | solution.py:467
  94.0 0.0 copy-start.1
  94.0 2.3 %copy.12 = bf16[1,128,4096]{2,1,0:T(8,128)(2,1)} copy(bf16[1,128,4096]{2,1,0:T(8,128)(2,1)} %bitcast.5) | data formatting | bytes 2097152
  96.3 0.0 copy-done.1
  96.3 0.0 copy-start
  96.3 0.7 copy.13
  97.0 0.3 copy-done
  97.2 0.7 copy.14
Async XLA Ops:
  94.0 2.3 %copy-start.1 = (bf16[512,128]{1,0:T(8,128)(2,1)S(1)}, bf16[512,128]{1,0:T(8,128)(2,1)}, u32[]{:S(2)}) copy-start(bf16[512,128]{1,0:T(8,128)(2,1)} %get-tuple-element.13) | copy-start | bytes 393220
  96.3 1.0 copy-start

commit v4 on v3

--- a/solution.py
+++ b/solution.py
@@ -40,7 +40,7 @@
     (0, 2), (2, 0), (2, 1), (1, 2), (2, 3), (3, 2), (2, 2),
 )
 FLOWS = ((0, 1, 4), (1, -1, 4), (0, -1, 3), (1, 1, 3))
-SUM_HOPS = {-1: 4, 1: 3}
+HOPS = {(t, way): hops for t, way, hops in FLOWS}
 
 
 def dot_t(a, b):
@@ -113,86 +113,69 @@
         row = pl.multiple_of(WIN + ((origin // 2) * 2 + side) * SHARD, SHARD)
         kt[origin % 2, :, pl.ds(row, SHARD)] = kv[0, origin % 2, pl.ds(row, SHARD), :].T
 
-    def ring_step(h, r):
-        far = (z + h) % 2
-        away = 2 * r - far
-        for f, (t, way, hops) in enumerate(FLOWS):
-            origin = (z + 2 * RING - way * away) % RING
-            here = slot(t, origin, core)
-
-            @pl.when(away <= hops)
-            def _():
-                ring_copy(f, away - 1, here, here).wait_recv()
-
-                @pl.when(away < hops)
-                def _():
-                    ring_copy(f, away, here, here).start()
-
-                side_copy(f, away - 1, here, here).start()
-
-        for f, (t, way, hops) in enumerate(FLOWS):
+    def origin_of(way, away):
+        return (z + RING - way * away) % RING
+
+    def ring_step(away):
+        flows = [(f, t, way, hops) for f, (t, way, hops) in enumerate(FLOWS) if away <= hops]
+        for f, t, way, hops in flows:
+            here = slot(t, origin_of(way, away), core)
+            ring_copy(f, away - 1, here, here).wait_recv()
+            if away < hops:
+                ring_copy(f, away, here, here).start()
+            side_copy(f, away - 1, here, here).start()
+        for f, t, way, hops in flows:
             if t == 0:
-                origin = (z + 2 * RING - way * away) % RING
-
-                @pl.when(away <= hops)
-                def _():
-                    turn(origin, core)
-
-    def side_wait(h):
-        far = (z + h) % 2
-
-        @pl.when(far == 0)
-        def _():
+                turn(origin_of(way, away), core)
+
+    def side_wait(away):
+        if away == 0:
             for t in range(2):
                 there = slot(t, z, 1 - core)
                 side_copy(4, t, there, there).wait_recv()
             turn(z, 1 - core)
-
-        for r in (1, 2):
-            away = 2 * r - far
-            for f, (t, way, hops) in enumerate(FLOWS):
-                origin = (z + 2 * RING - way * away) % RING
-                there = slot(t, origin, 1 - core)
-
-                @pl.when(away <= hops)
-                def _():
-                    side_copy(f, away - 1, there, there).wait_recv()
-                    if t == 0:
-                        turn(origin, 1 - core)
+            return
+        for f, (t, way, hops) in enumerate(FLOWS):
+            if away <= hops:
+                there = slot(t, origin_of(way, away), 1 - core)
+                side_copy(f, away - 1, there, there).wait_recv()
+                if t == 0:
+                    turn(origin_of(way, away), 1 - core)
+
+    heads = (1 - z_lo, z_lo)
 
     mine = pl.multiple_of(col * BLK, BLK)
 
-    def cross(h):
+    def cross(order):
+        h = heads[order]
         for i, (dx, dy) in enumerate(MOVES):
             for t, src in enumerate((q_in, g_in)):
                 to = ((x + dx) % SIDE) * SIDE + (y + dy) % SIDE
                 yield remote(
                     src.at[:, pl.ds(pl.multiple_of((to * 2 + h) * HD, HD), HD)],
-                    qg.at[h, t, pl.ds(mine, BLK), :],
-                    x_send.at[h, t, i],
-                    x_recv.at[h, t, i],
+                    qg.at[order, t, pl.ds(mine, BLK), :],
+                    x_send.at[order, t, i],
+                    x_recv.at[order, t, i],
                     at_xy(dx, dy),
                 )
 
     local = []
     for t in range(2):
         local.append(pltpu.make_async_copy(own_kv[t], slot(t, z, core), own_sem.at[0, t]))
-    for h in range(2):
+    for order in range(2):
         for t, src in enumerate((q_in, g_in)):
             local.append(
                 pltpu.make_async_copy(
-                    src.at[:, pl.ds(pl.multiple_of((col * 2 + h) * HD, HD), HD)],
-                    qg.at[h, t, pl.ds(mine, BLK), :],
-                    own_sem.at[1 + h, t],
+                    src.at[:, pl.ds(pl.multiple_of((col * 2 + heads[order]) * HD, HD), HD)],
+                    qg.at[order, t, pl.ds(mine, BLK), :],
+                    own_sem.at[1 + order, t],
                 )
             )
 
-    @pl.when(z_lo == 1)
-    def _():
-        send_own()
-
-    for c in cross(1):
-        c.start()
+    send_own()
+    for order in range(2):
+        for c in cross(order):
+            c.start()
     for c in local:
         c.start()
     for h in range(2):
@@ -206,30 +189,13 @@
     for c in local:
         c.wait()
 
-    ring_step(1, 1)
-
-    @pl.when(z_lo == 0)
-    def _():
-        send_own()
-
     turn(z, core)
-
-    @pl.when(z_lo == 1)
-    def _():
-        ring_step(0, 1)
-
-    for c in cross(1):
-        c.wait_send()
+    ring_step(1)
+    ring_step(2)
+    ring_step(3)
+    side_wait(1)
+    side_wait(3)
     for c in cross(0):
-        c.start()
-    ring_step(1, 2)
-
-    @pl.when(z_lo == 0)
-    def _():
-        ring_step(0, 1)
-
-    side_wait(1)
-    for c in cross(1):
         c.wait_recv()
 
     quarter = depth // 2
@@ -244,8 +210,8 @@
             sib_out.at[target], sib_in.at[target], ss_send.at[target], ss_recv.at[target], sibling
         )
 
-    def swap(h, ahead):
-        target = ((quarter + ahead) % 4) * 2 + h
+    def swap(away):
+        target = (z + away) % RING
         for t in range(2):
             sib_out[target, t] = partial(t, target, 1 - core).astype(BF16)
         swap_copy(target).start()
@@ -260,21 +226,16 @@
             rs_send.at[f, left - 1], rs_recv.at[f, left - 1], along(way),
         )
 
-    def sum_round(h, far_round, way, near, add):
-        left = (4 if far_round else 2) - near
-
-        @pl.when((z + h) % 2 == near)
-        def _():
-            target = (z + RING + way * left) % RING
-            swap_copy(target).wait_recv()
-            for t in range(2):
-                f = 2 * t + (1 if way > 0 else 0)
-                value = chip_sum(t, target)
-                if add:
-                    sum_copy(t, way, left + 1).wait_recv()
-                    value += ring_in[f, left].astype(F32)
-                ring_out[f, left - 1] = value.astype(BF16)
-                sum_copy(t, way, left).start()
+    def sum_round(t, way, left):
+        value = chip_sum(t, (z + RING + way * left) % RING)
+        if left < HOPS[t, way]:
+            sum_copy(t, way, left + 1).wait_recv()
+            value += ring_in[2 * t + (1 if way > 0 else 0), left].astype(F32)
+        ring_out[2 * t + (1 if way > 0 else 0), left - 1] = value.astype(BF16)
+        sum_copy(t, way, left).start()
+
+    def swap_wait(away):
+        swap_copy((z + away) % RING).wait_recv()
 
     shift = off_ref[depth]
     span = win_ref[depth]
@@ -286,72 +247,57 @@
         def step(k):
             return pl.when(n == k)
 
-        @pl.when(n == 5 - 2 * z_lo)
-        def _():
-            ring_step(0, 2)
-
-        @step(5)
-        def _():
-            swap(1, 2)
-
-        @step(7)
-        def _():
-            swap(1, 3)
+        @step(4)
+        def _():
+            ring_step(4)
 
         @step(8)
         def _():
-            swap(1, 0)
-            swap(1, 1)
             side_wait(0)
-            for c in cross(0):
+            side_wait(2)
+            side_wait(4)
+            for c in cross(1):
                 c.wait_recv()
-
-        @step(9)
-        def _():
-            sum_round(1, True, -1, 0, False)
-            sum_round(1, True, 1, 1, False)
-
-        @step(11)
-        def _():
-            sum_round(1, True, -1, 1, True)
+            for away in (3, 5, 1, 7):
+                swap(away)
+
+        @step(10)
+        def _():
+            for away in (3, 5, 1, 7):
+                swap_wait(away)
+            sum_round(0, -1, 3)
+            sum_round(1, 1, 3)
 
         @step(12 + z_lo)
         def _():
-            swap(0, 2)
-
-        @step(12)
-        def _():
-            sum_round(1, False, 1, 0, True)
-
-        @step(13)
-        def _():
-            sum_round(1, False, -1, 0, True)
-            sum_round(0, True, -1, 0, False)
+            swap(4)
+
+        @step(13 + z_lo)
+        def _():
+            swap_wait(4)
+            sum_round(0, 1, 4)
+            sum_round(1, -1, 4)
 
         @step(14 + z_lo)
         def _():
-            swap(0, 3)
-
-        @step(14)
-        def _():
-            sum_round(0, True, 1, 1, False)
+            swap(6)
 
         @step(15)
         def _():
-            sum_round(1, False, 1, 1, True)
-            sum_round(1, False, -1, 1, True)
-            sum_round(0, True, -1, 1, True)
+            sum_round(0, 1, 3)
+            sum_round(1, -1, 3)
 
     def tile(n, carry):
         steps(n)
-        h = 1 - n // 8
+        order = n // 8
+        h = jnp.where(order == 0, heads[0], heads[1])
         u = (2 * quarter + 4 - z_lo + n) % 8
         base = pl.multiple_of((4 * u + z_lo) * BLK, BLK)
         low = jnp.maximum(last - span, WIN - 1 - base)
         high = jnp.minimum(last, TOTAL + WIN - 1 - base)
         rows_q = pl.multiple_of(u * 2 * BLK, 2 * BLK)
-        q = qg[h, 0, pl.ds(rows_q, 2 * BLK), :]
-        g = qg[h, 1, pl.ds(rows_q, 2 * BLK), :]
+        q = qg[order, 0, pl.ds(rows_q, 2 * BLK), :]
+        g = qg[order, 1, pl.ds(rows_q, 2 * BLK), :]
 
         def join(part, value, halves, op):
             c0, n0 = COLS[halves]
@@ -418,12 +364,18 @@
 
     lax.fori_loop(0, 16, tile, 0)
 
-    swap(0, 1)
-    swap(0, 0)
-    sum_round(0, False, -1, 0, True)
-    sum_round(0, False, 1, 0, True)
-    sum_round(0, False, -1, 1, True)
-    sum_round(0, False, 1, 1, True)
+    swap(2)
+    swap(0)
+    swap_wait(6)
+    sum_round(0, -1, 2)
+    sum_round(1, -1, 2)
+    swap_wait(2)
+    sum_round(1, 1, 2)
+    sum_round(0, 1, 2)
+    for t in range(2):
+        sum_round(t, -1, 1)
+    for t in (1, 0):
+        sum_round(t, 1, 1)
     swap_copy(z).wait_recv()
     for t, dst in enumerate((dk_out, dv_out)):
         value = chip_sum(t, z)
@@ -448,14 +400,14 @@
     for t in range(2):
         here = slot(t, z, core)
         side_copy(4, t, here, here).wait_send()
-    for c in cross(0):
-        c.wait_send()
+    for order in range(2):
+        for c in cross(order):
+            c.wait_send()
     for target in range(RING):
         swap_copy(target).wait_send()
-    for way, hops in SUM_HOPS.items():
-        for t in range(2):
-            for left in range(1, hops + 1):
-                sum_copy(t, way, left).wait_send()
+    for t, way, hops in FLOWS:
+        for left in range(1, hops + 1):
+            sum_copy(t, way, left).wait_send()
 
 
 def on_device(queries, grad_out, key_states, value_states, offsets, windows):

time: 98.1 us -> 87.6 us (0.89)
  Pallas kernels: 93.3 us -> 82.9 us
    pallas_call x1, Pallas kernels: 93.3 us -> 82.9 us  [on_device(): pl.pallas_call(fused_kernel, out_shape=(jax.ShapeDtypeStruct((rows, width...]
where the time goes in v4:
time: 87.6 us; the launch traced here: 87.4 us
  Pallas kernels  82.9 us (95%)
  local copies, waits for them, and re-layouts  3.93 us (4%)
    pallas_call x1, Pallas kernels, on_device(): pl.pallas_call(fused_kernel, out_shape=(jax.ShapeDtypeStruct((rows, width...  82.9 us
    unnamed x7, local copies, waits for them, and re-layouts  3.93 us

profile of v4, /device:TPU:1, one launch (start us, length us, event | category | flops | bytes accessed | tf_op | source)
XLA Modules:
  0.0 87.4 jit_solution(3824731222013155285)
XLA Ops:
  0.6 82.9 %shard_map.85 = (bf16[128,4096]{1,0:T(8,128)(2,1)}, bf16[512,128]{1,0:T(8,128)(2,1)}, bf16[512,128]{1,0:T(8,128)(2,1)}) custom-call(s32[8]{0:T(128)} %off_ref.1, s32[8]{0:T(128)} %win_ref.1, bf16[128,4096]{1,0:T(8,128)(2,1)} %bitcast.3, bf16[128,4096]{1,0:T(8,128)(2,1)} %bitcast.4, bf16[512,128]{1,0:T(8,128)(2,1)} %k_in.1, bf16[512,128]{1,0:T(8,128)(2,1)} %v_in.1), custom_call_target="tpu_custom_call" | custom-call | tf_op jit(solution)/shard_map/pallas_call | solution.py:419
  83.5 0.0 copy-start.1
  83.5 2.3 %copy.12 = bf16[1,128,4096]{2,1,0:T(8,128)(2,1)} copy(bf16[1,128,4096]{2,1,0:T(8,128)(2,1)} %bitcast.5) | data formatting | bytes 2097152
  85.8 0.0 copy-done.1
  85.8 0.0 copy-start
  85.8 0.7 copy.13
  86.5 0.3 copy-done
  86.8 0.7 copy.14
Async XLA Ops:
  83.5 2.3 %copy-start.1 = (bf16[512,128]{1,0:T(8,128)(2,1)S(1)}, bf16[512,128]{1,0:T(8,128)(2,1)}, u32[]{:S(2)}) copy-start(bf16[512,128]{1,0:T(8,128)(2,1)} %get-tuple-element.13) | copy-start | bytes 393220
  85.8 1.0 %copy-start = (bf16[512,128]{1,0:T(8,128)(2,1)S(1)}, bf16[512,128]{1,0:T(8,128)(2,1)}, u32[]{:S(2)}) copy-start(bf16[512,128]{1,0:T(8,128)(2,1)} %get-tuple-element.14) | copy-start | bytes 393220

commit v5 on v4

--- a/solution.py
+++ b/solution.py
@@ -54,7 +54,7 @@
 def fused_kernel(
     off_ref, win_ref, q_in, g_in, k_in, v_in,
     dq_out, dk_out, dv_out,
-    qg, kv, kt, acc, s_scr, dp_scr, ds_scr, dqs, sib_out, sib_in, ring_out, ring_in,
+    qg, kv, kt, acc, s_scr, s_scr2, dp_scr, ds_scr, dqs, sib_out, sib_in, ring_out, ring_in,
     x_send, x_recv, own_sem, ag_send, ag_recv, sb_send, sb_recv, dq_send, dq_recv, dq_own,
     ss_send, ss_recv, rs_send, rs_recv,
 ):
@@ -142,7 +142,7 @@
                 if t == 0:
                     turn(origin_of(way, away), 1 - core)
 
-    heads = (1 - z_lo, z_lo)
+    heads = (z_lo, 1 - z_lo)
 
     mine = pl.multiple_of(col * BLK, BLK)
 
@@ -173,11 +173,11 @@
             )
 
     send_own()
+    for c in local:
+        c.start()
     for order in range(2):
         for c in cross(order):
             c.start()
-    for c in local:
-        c.start()
     for h in range(2):
         for t in range(2):
             kv[t, h, pl.ds(0, WIN), :] = jnp.zeros((WIN, HD), BF16)
@@ -186,15 +186,14 @@
         kt[h, :, pl.ds(WIN + TOTAL, BLK)] = jnp.zeros((HD, BLK), BF16)
     acc[...] = jnp.zeros_like(acc)
     ds_scr[...] = jnp.zeros_like(ds_scr)
-    for c in local:
-        c.wait()
-
+    local[0].wait()
     turn(z, core)
     ring_step(1)
     ring_step(2)
-    ring_step(3)
-    side_wait(1)
-    side_wait(3)
+    side_wait(0)
+    side_wait(2)
+    for c in local[1:]:
+        c.wait()
     for c in cross(0):
         c.wait_recv()
 
@@ -243,84 +242,117 @@
     place = lane + jnp.where(lane >= BLK, BLK, 0)
     last = place + WIN + shift
 
+    def tile_of(n):
+        order = n // 8
+        h = jnp.where(order == 0, heads[0], heads[1])
+        return order, h, (2 * quarter + n + order * (2 + z_lo)) % 8
+
+    def send_dq(group, k):
+        m = (k + col) % 2
+        order, h, u = tile_of(group)
+        to = 2 * u + m
+        src = dqs.at[h, pl.ds(pl.multiple_of(to * BLK, BLK), BLK), :]
+        dst = dq_out.at[:, pl.ds(pl.multiple_of((col * 2 + h) * HD, HD), HD)]
+
+        @pl.when(to != col)
+        def _():
+            remote(src, dst, dq_send.at[h, to], dq_recv.at[h, col], (depth, to * 2 + z_lo)).start()
+
+        @pl.when(to == col)
+        def _():
+            pltpu.make_async_copy(src, dst, dq_own.at[h]).start()
+
     def steps(n):
         def step(k):
             return pl.when(n == k)
 
-        @step(4)
+        @step(1)
+        def _():
+            ring_step(3)
+
+        @step(2)
         def _():
             ring_step(4)
-
-        @step(8)
-        def _():
-            side_wait(0)
-            side_wait(2)
             side_wait(4)
+
+        @step(7)
+        def _():
+            side_wait(1)
+            side_wait(3)
             for c in cross(1):
                 c.wait_recv()
-            for away in (3, 5, 1, 7):
+
+        @step(8)
+        def _():
+            for away in (4, 2, 6, 0):
                 swap(away)
 
         @step(10)
-        def _():
-            for away in (3, 5, 1, 7):
-                swap_wait(away)
-            sum_round(0, -1, 3)
-            sum_round(1, 1, 3)
-
-        @step(12 + z_lo)
-        def _():
-            swap(4)
-
-        @step(13 + z_lo)
         def _():
             swap_wait(4)
             sum_round(0, 1, 4)
             sum_round(1, -1, 4)
 
+        @step(12 + z_lo)
+        def _():
+            swap(3)
+
+        @step(13 + z_lo)
+        def _():
+            swap_wait(3)
+            sum_round(1, 1, 3)
+            sum_round(0, 1, 3)
+
         @step(14 + z_lo)
         def _():
-            swap(6)
-
-        @step(15)
-        def _():
-            sum_round(0, 1, 3)
-            sum_round(1, -1, 3)
-
-    def tile(n, carry):
-        steps(n)
-        order = n // 8
-        h = jnp.where(order == 0, heads[0], heads[1])
-        u = (2 * quarter + 4 - z_lo + n) % 8
+            swap(5)
+
+        @step(15 + z_lo)
+        def _():
+            down_three()
+
+    def down_three():
+        swap_wait(5)
+        sum_round(0, -1, 3)
+        sum_round(1, -1, 3)
+
+    def join(part, value, halves, op):
+        if halves == "ab":
+            return op(part, value)
+        if halves == "a":
+            return jnp.concatenate([op(part[:, :BLK], value), part[:, BLK:]], axis=1)
+        return jnp.concatenate([part[:, :BLK], op(part[:, BLK:], value)], axis=1)
+
+    def place_of(n):
+        order, h, u = tile_of(n)
         base = pl.multiple_of((4 * u + z_lo) * BLK, BLK)
-        low = jnp.maximum(last - span, WIN - 1 - base)
-        high = jnp.minimum(last, TOTAL + WIN - 1 - base)
         rows_q = pl.multiple_of(u * 2 * BLK, 2 * BLK)
+        return order, h, base, rows_q
+
+    def score_block(n, s_scr, block, top):
+        k0, rows, halves, bound = block
+        c0, cn = COLS[halves]
+        order, h, base, rows_q = place_of(n)
+        q = qg[order, 0, pl.ds(rows_q, 2 * BLK), :]
+        s = dot_t(kv[0, h, pl.ds(pl.multiple_of(base + k0, 16), rows), :], q[c0 : c0 + cn])
+        if bound is not None:
+            key = lax.broadcasted_iota(jnp.int32, (rows, cn), 0)
+            if bound == "low":
+                low = jnp.maximum(last - span, WIN - 1 - base)
+                keep = key > low[:, c0 : c0 + cn] - k0
+            else:
+                high = jnp.minimum(last, TOTAL + WIN - 1 - base)
+                keep = key <= high[:, c0 : c0 + cn] - k0
+            s = jnp.where(keep, s, NEG)
+        s_scr[pl.ds(k0, rows), pl.ds(c0, cn)] = s
+        return join(top, jnp.max(s, axis=0, keepdims=True), halves, jnp.maximum)
+
+    lowest = jnp.full((1, 2 * BLK), NEG, F32)
+
+    def tile(n, s_scr, top, after, s_after):
+        order, h, base, rows_q = place_of(n)
         q = qg[order, 0, pl.ds(rows_q, 2 * BLK), :]
         g = qg[order, 1, pl.ds(rows_q, 2 * BLK), :]
-
-        def join(part, value, halves, op):
-            c0, n0 = COLS[halves]
-            if halves == "ab":
-                return op(part, value)
-            if halves == "a":
-                return jnp.concatenate([op(part[:, :BLK], value), part[:, BLK:]], axis=1)
-            return jnp.concatenate([part[:, :BLK], op(part[:, BLK:], value)], axis=1)
-
-        top = jnp.full((1, 2 * BLK), NEG, F32)
-        for k0, rows, halves, bound in BLOCKS:
-            c0, cn = COLS[halves]
-            at = pl.multiple_of(base + k0, 16)
-            s = dot_t(kv[0, h, pl.ds(at, rows), :], q[c0 : c0 + cn])
-            if bound is not None:
-                key = lax.broadcasted_iota(jnp.int32, (rows, cn), 0)
-                if bound == "low":
-                    keep = key > low[:, c0 : c0 + cn] - k0
-                else:
-                    keep = key <= high[:, c0 : c0 + cn] - k0
-                s = jnp.where(keep, s, NEG)
-            s_scr[pl.ds(k0, rows), pl.ds(c0, cn)] = s
-            top = join(top, jnp.max(s, axis=0, keepdims=True), halves, jnp.maximum)
         top = top * SCALE2
         sum_e = jnp.zeros((1, 2 * BLK), F32)
         sum_d = jnp.zeros((1, 2 * BLK), F32)
@@ -335,47 +367,63 @@
             dp_scr[pl.ds(k0, rows), pl.ds(c0, cn)] = dp
         inv = 1.0 / sum_e
         rowdot = sum_d * inv
-        for k0, rows, halves, bound in BLOCKS:
+        new_top = lowest
+        for block in BLOCKS:
+            k0, rows, halves, bound = block
             c0, cn = COLS[halves]
             at = pl.multiple_of(base + k0, 16)
             p = s_scr[pl.ds(k0, rows), pl.ds(c0, cn)] * inv[:, c0 : c0 + cn]
             ds = p * (dp_scr[pl.ds(k0, rows), pl.ds(c0, cn)] - rowdot[:, c0 : c0 + cn])
             ds = ds.astype(BF16)
             ds_scr[pl.ds(k0, rows), pl.ds(c0, cn)] = ds
+            new_top = score_block(after, s_after, block, new_top)
             acc[1, h, pl.ds(at, rows), :] += dot(p.astype(BF16), g[c0 : c0 + cn])
             acc[0, h, pl.ds(at, rows), :] += dot(ds, q[c0 : c0 + cn])
         dqt = dot(kt[h, :, pl.ds(base, TAIL)], ds_scr[...])
         dqs[h, pl.ds(rows_q, 2 * BLK), :] = (dqt.T * SCALE).astype(BF16)
-
-        for half in range(2):
-            to = 2 * u + half
-            src = dqs.at[h, pl.ds(pl.multiple_of(to * BLK, BLK), BLK), :]
-            dst = dq_out.at[:, pl.ds(pl.multiple_of((col * 2 + h) * HD, HD), HD)]
-
-            @pl.when(to != col)
-            def _():
-                remote(src, dst, dq_send.at[h, to], dq_recv.at[h, col], (depth, to * 2 + z_lo)).start()
-
-            @pl.when(to == col)
-            def _():
-                pltpu.make_async_copy(src, dst, dq_own.at[h]).start()
-
-        return carry
-
-    lax.fori_loop(0, 16, tile, 0)
-
-    swap(2)
-    swap(0)
+        return new_top
+
+    def before(n):
+        steps(n)
+
+        @pl.when(n >= 1)
+        def _():
+            for b in range(2):
+                send_dq(n - 1, b)
+
+    def pair(i, top):
+        n = 2 * i
+        before(n)
+        top = tile(n, s_scr, top, n + 1, s_scr2)
+        before(n + 1)
+        return tile(n + 1, s_scr2, top, jnp.minimum(n + 2, 15), s_scr)
+
+    first = lowest
+    for block in BLOCKS:
+        first = score_block(0, s_scr, block, first)
+    lax.fori_loop(0, 8, pair, first)
+
+    swap(1)
+    swap(7)
+
+    @pl.when(z_lo == 1)
+    def _():
+        down_three()
+
+    swap_wait(2)
     swap_wait(6)
+    sum_round(1, 1, 2)
+    sum_round(0, 1, 2)
+    for k in range(2):
+        send_dq(15, k)
     sum_round(0, -1, 2)
     sum_round(1, -1, 2)
-    swap_wait(2)
-    sum_round(1, 1, 2)
-    sum_round(0, 1, 2)
-    for t in range(2):
-        sum_round(t, -1, 1)
-    for t in (1, 0):
-        sum_round(t, 1, 1)
+    swap_wait(1)
+    sum_round(1, 1, 1)
+    sum_round(0, 1, 1)
+    swap_wait(7)
+    sum_round(0, -1, 1)
+    sum_round(1, -1, 1)
     swap_copy(z).wait_recv()
     for t, dst in enumerate((dk_out, dv_out)):
         value = chip_sum(t, z)
@@ -432,6 +480,7 @@
             pltpu.VMEM((2, 2, PAD, HD), F32),
             pltpu.VMEM((SPAN, 2 * BLK), F32),
             pltpu.VMEM((SPAN, 2 * BLK), F32),
+            pltpu.VMEM((SPAN, 2 * BLK), F32),
             pltpu.VMEM((TAIL, 2 * BLK), BF16),
             pltpu.VMEM((2, PEERS * BLK, HD), BF16),
             pltpu.VMEM((RING, 2, SHARD, HD), BF16),

time: 87.6 us -> 83.1 us (0.949)
  Pallas kernels: 82.9 us -> 78.4 us
    pallas_call x1, Pallas kernels: 82.9 us -> 78.4 us  [on_device(): pl.pallas_call(fused_kernel, out_shape=(jax.ShapeDtypeStruct((rows, width...]
where the time goes in v5:
time: 83.1 us; the launch traced here: 83 us
  Pallas kernels  78.4 us (94%)
  local copies, waits for them, and re-layouts  3.93 us (5%)
    pallas_call x1, Pallas kernels, on_device(): pl.pallas_call(fused_kernel, out_shape=(jax.ShapeDtypeStruct((rows, width...  78.4 us
    unnamed x7, local copies, waits for them, and re-layouts  3.93 us

profile of v5, /device:TPU:1, one launch (start us, length us, event | category | flops | bytes accessed | tf_op | source)
XLA Modules:
  0.0 83.0 jit_solution(10642301824908282772)
XLA Ops:
  0.6 78.4 %shard_map.85 = (bf16[128,4096]{1,0:T(8,128)(2,1)}, bf16[512,128]{1,0:T(8,128)(2,1)}, bf16[512,128]{1,0:T(8,128)(2,1)}) custom-call(s32[8]{0:T(128)} %off_ref.1, s32[8]{0:T(128)} %win_ref.1, bf16[128,4096]{1,0:T(8,128)(2,1)} %bitcast.3, bf16[128,4096]{1,0:T(8,128)(2,1)} %bitcast.4, bf16[512,128]{1,0:T(8,128)(2,1)} %k_in.1, bf16[512,128]{1,0:T(8,128)(2,1)} %v_in.1), custom_call_target="tpu_custom_call" | custom-call | tf_op jit(solution)/shard_map/pallas_call | solution.py:467
  79.0 0.0 copy-start.1
  79.0 2.3 %copy.12 = bf16[1,128,4096]{2,1,0:T(8,128)(2,1)} copy(bf16[1,128,4096]{2,1,0:T(8,128)(2,1)} %bitcast.5) | data formatting | bytes 2097152
  81.4 0.0 copy-done.1
  81.4 0.0 copy-start
  81.4 0.7 copy.13
  82.0 0.3 copy-done
  82.3 0.7 copy.14
Async XLA Ops:
  79.0 2.3 %copy-start.1 = (bf16[512,128]{1,0:T(8,128)(2,1)S(1)}, bf16[512,128]{1,0:T(8,128)(2,1)}, u32[]{:S(2)}) copy-start(bf16[512,128]{1,0:T(8,128)(2,1)} %get-tuple-element.13) | copy-start | bytes 393220
  81.4 1.0 %copy-start = (bf16[512,128]{1,0:T(8,128)(2,1)S(1)}, bf16[512,128]{1,0:T(8,128)(2,1)}, u32[]{:S(2)}) copy-start(bf16[512,128]{1,0:T(8,128)(2,1)} %get-tuple-element.14) | copy-start | bytes 393220

commit v6 on v5

--- a/solution.py
+++ b/solution.py
@@ -272,13 +272,13 @@
 
         @step(2)
         def _():
+            side_wait(1)
+            side_wait(3)
             ring_step(4)
             side_wait(4)
 
         @step(7)
         def _():
-            side_wait(1)
-            side_wait(3)
             for c in cross(1):
                 c.wait_recv()
 
@@ -287,7 +287,7 @@
             for away in (4, 2, 6, 0):
                 swap(away)
 
-        @step(10)
+        @step(9)
         def _():
             swap_wait(4)
             sum_round(0, 1, 4)
@@ -307,7 +307,7 @@
         def _():
             swap(5)
 
-        @step(15 + z_lo)
+        @step(15)
         def _():
             down_three()
 
@@ -376,11 +376,12 @@
             ds = p * (dp_scr[pl.ds(k0, rows), pl.ds(c0, cn)] - rowdot[:, c0 : c0 + cn])
             ds = ds.astype(BF16)
             ds_scr[pl.ds(k0, rows), pl.ds(c0, cn)] = ds
-            new_top = score_block(after, s_after, block, new_top)
+            if s_after is not None:
+                new_top = score_block(after, s_after, block, new_top)
             acc[1, h, pl.ds(at, rows), :] += dot(p.astype(BF16), g[c0 : c0 + cn])
             acc[0, h, pl.ds(at, rows), :] += dot(ds, q[c0 : c0 + cn])
         dqt = dot(kt[h, :, pl.ds(base, TAIL)], ds_scr[...])
-        dqs[h, pl.ds(rows_q, 2 * BLK), :] = (dqt.T * SCALE).astype(BF16)
+        dqs[h, pl.ds(rows_q, 2 * BLK), :] = (dqt.T * (2 * SCALE)).astype(BF16)
         return new_top
 
     def before(n):
@@ -396,19 +397,19 @@
         before(n)
         top = tile(n, s_scr, top, n + 1, s_scr2)
         before(n + 1)
-        return tile(n + 1, s_scr2, top, jnp.minimum(n + 2, 15), s_scr)
+        return tile(n + 1, s_scr2, top, n + 2, s_scr)
 
     first = lowest
     for block in BLOCKS:
         first = score_block(0, s_scr, block, first)
-    lax.fori_loop(0, 8, pair, first)
+    top = lax.fori_loop(0, 7, pair, first)
+    before(jnp.int32(14))
+    top = tile(jnp.int32(14), s_scr, top, jnp.int32(15), s_scr2)
+    before(jnp.int32(15))
+    tile(jnp.int32(15), s_scr2, top, None, None)
 
     swap(1)
     swap(7)
-
-    @pl.when(z_lo == 1)
-    def _():
-        down_three()
 
     swap_wait(2)
     swap_wait(6)
@@ -430,7 +431,7 @@
         for way in (-1, 1):
             sum_copy(t, way, 1).wait_recv()
             value += ring_in[2 * t + (1 if way > 0 else 0), 0].astype(F32)
-        dst[...] = value.astype(BF16)
+        dst[...] = (value * 2).astype(BF16)
 
     for h in range(2):
         dst = dq_out.at[:, pl.ds(pl.multiple_of((col * 2 + h) * HD, HD), HD)]
@@ -499,7 +500,8 @@
         offsets, windows, queries.reshape(rows, width), grad_out.reshape(rows, width),
         key_states, value_states,
     )
-    return dq.reshape(1, rows, width), dk, dv
+    half = jnp.asarray(0.5, BF16)
+    return (dq * half).reshape(1, rows, width), dk * half, dv * half
 
 
 def solution(mesh):

time: 83.1 us -> 81.5 us (0.981)
  local copies, waits for them, and re-layouts: 3.93 us -> 0.01 us
  other arithmetic: 0 us -> 3.05 us
    unnamed x7 -> x4, local copies, waits for them, and re-layouts: 3.93 us -> 0.01 us
    reshape x0 -> x1, other arithmetic: none -> 2.33 us  [on_device(): return ((dq * half).reshape(1, rows, width), dk * half, dv * half)]
where the time goes in v6:
time: 81.5 us; the launch traced here: 81.3 us
  Pallas kernels  77.6 us (95%)
  other arithmetic  3.05 us (4%)
    pallas_call x1, Pallas kernels, on_device(): pl.pallas_call(fused_kernel, out_shape=(jax.ShapeDtypeStruct((rows, width...  77.6 us
    reshape x1, other arithmetic, on_device(): return ((dq * half).reshape(1, rows, width), dk * half, dv * half)  2.33 us

profile of v6, /device:TPU:1, one launch (start us, length us, event | category | flops | bytes accessed | tf_op | source)
XLA Modules:
  0.0 81.3 jit_solution(4955285048717975974)
XLA Ops:
  0.6 77.6 %shard_map.85 = (bf16[128,4096]{1,0:T(8,128)(2,1)}, bf16[512,128]{1,0:T(8,128)(2,1)}, bf16[512,128]{1,0:T(8,128)(2,1)}) custom-call(s32[8]{0:T(128)} %off_ref.1, s32[8]{0:T(128)} %win_ref.1, bf16[128,4096]{1,0:T(8,128)(2,1)} %bitcast.4, bf16[128,4096]{1,0:T(8,128)(2,1)} %bitcast.5, bf16[512,128]{1,0:T(8,128)(2,1)} %k_in.1, bf16[512,128]{1,0:T(8,128)(2,1)} %v_in.1), custom_call_target="tpu_custom_call" | custom-call | tf_op jit(solution)/shard_map/pallas_call | solution.py:468
  78.3 0.0 copy-start
  78.3 0.0 copy-start.1
  78.3 2.3 %multiply_bitcast_fusion = bf16[1,128,4096]{2,1,0:T(8,128)(2,1)} fusion(bf16[128,4096]{1,0:T(8,128)(2,1)} %get-tuple-element.6), kind=kLoop, calls=%fused_computation | loop fusion | flops 524288 | bytes 2097152 | tf_op jit(solution)/shard_map/reshape | solution.py:504
  80.6 0.0 copy-done
  80.6 0.0 copy-done.1
  80.6 0.7 broadcast_multiply_fusion
Async XLA Ops:
  78.3 2.4 %copy-start = (bf16[512,128]{1,0:T(8,128)(2,1)S(1)}, bf16[512,128]{1,0:T(8,128)(2,1)}, u32[]{:S(2)}) copy-start(bf16[512,128]{1,0:T(8,128)(2,1)} %get-tuple-element.7) | copy-start | bytes 393220
  78.3 2.3 %copy-start.1 = (bf16[512,128]{1,0:T(8,128)(2,1)S(1)}, bf16[512,128]{1,0:T(8,128)(2,1)}, u32[]{:S(2)}) copy-start(bf16[512,128]{1,0:T(8,128)(2,1)} %get-tuple-element.8) | copy-start | bytes 393220
